TPU v7x, 512 devices: a whole 4x8x8 slice. The times are simulated.
512 devices in a mesh: ctx: 32 (over y, x), tp: 16 (over z, core).
Axes of the slice: x: 4, y: 8, z: 8, core: 2. Of those that a mesh axis runs over, the one named last changes fastest.
Arguments:
- query_rows: bfloat16 [8192, 8192], P('ctx', 'tp'), may hold values from -15 to 15
- key_rows: bfloat16 [8192, 8192], P('ctx', 'tp'), may hold values from -6 to 6
- value_rows: bfloat16 [8192, 8192], P('ctx', 'tp'), may hold values from -54 to 54
- log_decay: float32 [64, 8192], P('tp', 'ctx'), may hold values from -1.6 to 0
- norm_gain: float32 [8192], P('tp'), may hold values from 0.1 to 1.9
- d_normed: bfloat16 [8192, 8192], P('ctx', 'tp'), may hold values from -6 to 6
Outputs:
- d_queries: bfloat16 [8192, 8192], P('ctx', 'tp')
- d_keys: bfloat16 [8192, 8192], P('ctx', 'tp')
- d_values: bfloat16 [8192, 8192], P('ctx', 'tp')
All inputs are finite; a program needn't handle non-finite values.
Results may differ from a plain program's by a relative error of at most 0.01.
Values sent between devices are 32-bit elements; how exact they have to be, the bound alone decides.
No kernel may reach another device: no remote copies, remote signals or barrier semaphores. Data moves between devices by JAX's collectives and lax.ppermute only.
A program may use at most 64 MiB of HBM per device.

v0:
```python
import jax
import jax.numpy as jnp
from jax import lax
from jax.sharding import PartitionSpec as P

HEADS = 64
DK = 128
BLOCK = 256


EPSILON = 1e-06


def prefix(array, axis, combine, identity, reverse):
    size, here = (lax.axis_size(axis), lax.axis_index(axis))
    everything = jax.tree.map(lambda part: lax.all_gather(part, axis), array)
    start = jax.tree.map(
        lambda part, zero: jnp.broadcast_to(jnp.asarray(zero, part.dtype), part.shape),
        array,
        identity,
    )

    def lap(k, before):
        at = size - 1 - k if reverse else k
        reached = at > here if reverse else at < here
        new = combine(before, jax.tree.map(lambda part: part[at], everything))
        return jax.tree.map(lambda a, b: jnp.where(reached, a, b), new, before)

    return lax.fori_loop(0, size, lap, start)


def carry_on(earlier, latter):
    fade_early, state_early = earlier
    fade_late, state_late = latter
    return (fade_early * fade_late, fade_late[..., None, None] * state_early + state_late)


def forward_step(carried, inputs_now):
    fade_now, update_now = inputs_now
    return (fade_now[:, None, None] * carried + update_now, carried)


def shards(query_rows, key_rows, value_rows, log_decay, norm_gain, d_normed):
    heads_here = log_decay.shape[0]
    nblocks = query_rows.shape[0] // BLOCK
    shape_four = (nblocks, BLOCK, heads_here, DK)
    queries = query_rows.reshape(shape_four)
    keyset = key_rows.reshape(shape_four)
    valueset = value_rows.reshape(shape_four)
    within = jnp.transpose(
        jnp.cumsum(log_decay.reshape(heads_here, nblocks, BLOCK), axis=2), (1, 0, 2)
    )
    totals = within[:, :, -1]
    token_offset = jnp.arange(BLOCK)
    causal = token_offset[:, None] >= token_offset[None, :]
    spread = within[:, :, :, None] - within[:, :, None, :]
    decay_mask = jnp.where(causal, jnp.exp(jnp.minimum(spread, 0.0)), 0.0)
    rise_scale = jnp.transpose(jnp.exp(within), (0, 2, 1))[..., None]
    fall_scale = jnp.transpose(jnp.exp(totals[:, :, None] - within), (0, 2, 1))[..., None]
    q_decayed = (queries * rise_scale).astype(jnp.bfloat16)
    k_decayed = (keyset * fall_scale).astype(jnp.bfloat16)
    scores = jnp.einsum("bthd,bshd->bhts", queries, keyset, preferred_element_type=jnp.float32)
    scored = (scores * decay_mask).astype(jnp.bfloat16)
    updates = jnp.einsum("bshd,bshe->bhde", k_decayed, valueset, preferred_element_type=jnp.float32)
    fade_block = jnp.exp(totals)
    zero_state = jnp.zeros((heads_here, DK, DK), jnp.float32)
    local_final, local_before = lax.scan(forward_step, zero_state, (fade_block, updates))
    device_fade = jnp.exp(jnp.sum(totals, axis=0))
    running_total = jnp.cumsum(totals, axis=0)
    lead_fade = jnp.exp(running_total - totals)
    tail_fade = jnp.exp(running_total - running_total)
    identity = (jnp.ones_like(device_fade), zero_state)
    incoming = prefix((device_fade, local_final), "ctx", carry_on, identity, False)[1]
    states = local_before + lead_fade[:, :, None, None] * incoming[None]
    states_low = states.astype(jnp.bfloat16)
    attended = jnp.einsum("bhts,bshd->bthd", scored, valueset, preferred_element_type=jnp.float32)
    attended = attended + jnp.einsum(
        "bthd,bhde->bthe", q_decayed, states_low, preferred_element_type=jnp.float32
    )
    attended = attended.astype(jnp.bfloat16)
    attended_wide = attended.astype(jnp.float32)
    gained = norm_gain.reshape(heads_here, DK) * d_normed.reshape(shape_four).astype(jnp.float32)
    squares = jnp.sum(attended_wide * attended_wide, axis=(2, 3))
    inner_sums = jnp.sum(attended_wide * gained, axis=(2, 3))
    squares, inner_sums = lax.psum((squares, inner_sums), "tp")
    features = HEADS * DK
    inv_rms = lax.rsqrt(squares / features + EPSILON)
    d_attended = (
        inv_rms[:, :, None, None] * gained
        - attended_wide * (inv_rms**3 * inner_sums / features)[:, :, None, None]
    ).astype(jnp.bfloat16)
    grads_in = jnp.einsum(
        "bthd,bthe->bhde", q_decayed, d_attended, preferred_element_type=jnp.float32
    )
    local_start, local_after = lax.scan(
        forward_step, zero_state, (fade_block, grads_in), reverse=True
    )
    outgoing = prefix((device_fade, local_start), "ctx", carry_on, identity, True)[1]
    gradients = local_after + tail_fade[:, :, None, None] * outgoing[None]
    grads_low = gradients.astype(jnp.bfloat16)
    d_scores = jnp.einsum(
        "bthe,bshe->bhts", d_attended, valueset, preferred_element_type=jnp.float32
    )
    d_scored = (d_scores * decay_mask).astype(jnp.bfloat16)
    d_query = jnp.einsum("bhts,bshd->bthd", d_scored, keyset, preferred_element_type=jnp.float32)
    d_query = d_query + rise_scale * jnp.einsum(
        "bthe,bhde->bthd", d_attended, states_low, preferred_element_type=jnp.float32
    )
    d_key = jnp.einsum("bhts,bthd->bshd", d_scored, queries, preferred_element_type=jnp.float32)
    d_key = d_key + fall_scale * jnp.einsum(
        "bshe,bhde->bshd", valueset, grads_low, preferred_element_type=jnp.float32
    )
    d_value = jnp.einsum("bhts,bthe->bshe", scored, d_attended, preferred_element_type=jnp.float32)
    d_value = d_value + jnp.einsum(
        "bshd,bhde->bshe", k_decayed, grads_low, preferred_element_type=jnp.float32
    )
    flat_shape = (nblocks * BLOCK, heads_here * DK)
    return (
        d_query.astype(jnp.bfloat16).reshape(flat_shape),
        d_key.astype(jnp.bfloat16).reshape(flat_shape),
        d_value.astype(jnp.bfloat16).reshape(flat_shape),
    )


def solution(mesh):
    placed = (
        P("ctx", "tp"),
        P("ctx", "tp"),
        P("ctx", "tp"),
        P("tp", "ctx"),
        P("tp"),
        P("ctx", "tp"),
    )
    return jax.shard_map(
        shards,
        mesh=mesh,
        in_specs=placed,
        out_specs=(P("ctx", "tp"), P("ctx", "tp"), P("ctx", "tp")),
        check_vma=False,
    )
```

profile of v0, /device:TPU:1, one launch (start us, length us, event | category | flops | bytes accessed | tf_op | source)
XLA Modules:
  0.0 326.5 jit_solution(18115912106437750562)
XLA Ops:
  8.0 1.2 reduce-window.6
  9.8 2.1 convolution_add_fusion.3
  12.1 31.4 %all-gather = f32[32,4,1]{1,2,0:T(1,128)S(1)} all-gather(f32[1,4,1]{1,2,0:T(1,128)S(1)} %copy.71), channel_id=2, replica_groups=mesh['ctx'=32,'tp'=16] {'ctx'}, dimensions={0}, use_global_device_ids=true | all-gather | bytes 528 | tf_op jit(solution)/shard_map/all_gather | solution.py:16
  43.7 1.1 copy.100
  44.7 1.1 copy.80
  46.4 1.3 convolution_bitcast_fusion.4
  47.7 73.0 %all-gather.6.cloned.1.call-done = f32[128,128,128]{2,1,0:T(8,128)} async-done(((f32[4,128,128]{2,1,0:T(8,128)}), f32[128,128,128]{2,1,0:T(8,128)}) %all-gather.6.cloned.1.call-update) | async-done | bytes 8388624 | tf_op jit(solution)/shard_map/all_gather | solution.py:16
  120.7 35.1 %while.40 = (s32[]{:T(128)}, f32[4,128,128]{2,1,0:T(8,128)S(1)}, s32[]{:T(128)}, f32[32,4]{1,0:T(8,128)S(1)}, f32[32,4,128,128]{3,2,1,0:T(8,128)}, /*index=5*/s32[]{:T(128)}, s32[]{:T(128)}) while((s32[]{:T(128)}, f32[4,128,128]{2,1,0:T(8,128)S(1)}, s32[]{:T(128)}, f32[32,4]{1,0:T(8,128)S(1)}, f32[32,4,128,128]{3,2,1,0:T(8,128)}, ...), condition=%wide.region_3.4_spmd.clone, body=%wide.region_2.3_spmd.clone.sunk | while | flops 262148 | bytes 786593 | solution.py:29
  121.8 1.1 fusion.53
  122.9 1.1 fusion.53
  124.0 1.1 fusion.53
  125.1 1.1 fusion.53
  126.2 1.1 fusion.53
  127.2 1.1 fusion.53
  128.3 1.1 fusion.53
  129.4 1.1 fusion.53
  130.5 1.1 fusion.53
  131.6 1.1 fusion.53
  132.7 1.1 fusion.53
  133.8 1.1 fusion.53
  134.9 1.1 fusion.53
  136.0 1.1 fusion.53
  137.1 1.1 fusion.53
  138.2 1.1 fusion.53
  139.3 1.1 fusion.53
  140.4 1.1 fusion.53
  141.5 1.1 fusion.53
  142.6 1.1 fusion.53
  143.7 1.1 fusion.53
  144.8 1.1 fusion.53
  145.9 1.1 fusion.53
  147.0 1.1 fusion.53
  148.1 1.1 fusion.53
  149.2 1.1 fusion.53
  150.3 1.1 fusion.53
  151.4 1.1 fusion.53
  152.5 1.1 fusion.53
  153.6 1.1 fusion.53
  154.7 1.1 fusion.53
  156.2 25.1 %all-reduce = (f32[1,256]{1,0:T(1,128)S(1)}, f32[1,256]{1,0:T(1,128)S(1)}) all-reduce(f32[1,256]{1,0:T(1,128)S(1)} %bitcast.173, f32[1,256]{1,0:T(1,128)S(1)} %bitcast.172), channel_id=1, replica_groups=mesh['ctx'=32,'tp'=16] {'tp'}, use_global_device_ids=true, to_apply=%region_7.8 | all-reduce | flops 512 | bytes 4096 | tf_op jit(solution)/shard_map/psum | solution.py:85
  184.8 97.2 %all-gather.8.cloned.1.call-done = f32[128,128,128]{2,1,0:T(8,128)} async-done(((f32[4,128,128]{2,1,0:T(8,128)}), f32[128,128,128]{2,1,0:T(8,128)}) %all-gather.8.cloned.1.call-update) | async-done | bytes 8388624 | tf_op jit(solution)/shard_map/all_gather | solution.py:16
  282.0 35.3 %while.41 = (s32[]{:T(128)}, f32[4,128,128]{2,1,0:T(8,128)S(1)}, s32[]{:T(128)}, f32[32,4]{1,0:T(8,128)S(1)}, f32[32,4,128,128]{3,2,1,0:T(8,128)}, /*index=5*/s32[]{:T(128)}, s32[]{:T(128)}, s32[]{:T(128)}, s32[]{:T(128)}) while((s32[]{:T(128)}, f32[4,128,128]{2,1,0:T(8,128)S(1)}, s32[]{:T(128)}, f32[32,4]{1,0:T(8,128)S(1)}, ...), condition=%wide.region_9.10_spmd.clone, body=%wide.region_8.9_spmd.clone.sunk | while | flops 262152 | bytes 786655 | solution.py:29
  283.1 1.1 fusion.54
  284.2 1.1 fusion.54
  285.3 1.1 fusion.54
  286.4 1.1 fusion.54
  287.5 1.1 fusion.54
  288.6 1.1 fusion.54
  289.7 1.1 fusion.54
  290.8 1.1 fusion.54
  291.9 1.1 fusion.54
  293.0 1.1 fusion.54
  294.1 1.1 fusion.54
  295.2 1.1 fusion.54
  296.3 1.1 fusion.54
  297.4 1.1 fusion.54
  298.5 1.1 fusion.54
  299.7 1.1 fusion.54
  301.9 1.1 fusion.54
  303.0 1.1 fusion.54
  307.4 1.1 fusion.54
  308.5 1.1 fusion.54
  312.9 1.1 fusion.54
  314.0 1.1 fusion.54
  (117 shorter events, 20.7 us)
Async XLA Ops:
  7.2 2.6 copy-start
  7.2 175.2 %copy-start.1 = (bf16[256,512]{1,0:T(8,128)(2,1)S(1)}, bf16[256,512]{1,0:T(8,128)(2,1)}, u32[]{:S(2)}) copy-start(bf16[256,512]{1,0:T(8,128)(2,1)} %param.12) | copy-start | bytes 786436
  7.2 148.6 %copy-start.2 = (f32[512]{0:T(512)S(1)}, f32[512]{0:T(512)}, u32[]{:S(2)}) copy-start(f32[512]{0:T(512)} %param.14) | copy-start | bytes 6148
  7.2 113.5 %all-gather.6.cloned.1.call-start = ((), (), s32[]{:S(2)}) async-start(), calls=%async_computation | async-start | bytes 8650752 | tf_op jit(solution)/shard_map/all_gather | solution.py:16
  11.9 270.1 %all-gather.8.cloned.1.call-start = ((), (), s32[]{:S(2)}) async-start(), calls=%async_computation.1 | async-start | bytes 8650752 | tf_op jit(solution)/shard_map/all_gather | solution.py:16
Sparse Core Ops, SparseCore 0:
  12.1 108.5 all-gather.5
  182.5 99.4 all-gather.7
where the time goes:
time: 329 us; the launch traced here: 327 us
  waiting for transfers between devices  170 us (52%)
  other arithmetic  69.2 us (21%)
  blocking collectives  56.5 us (17%)
  between operations  14.2 us (4%)
  matrix products  7.35 us (2%)
  local copies, waits for them, and re-layouts  6.73 us (2%)
    all_gather x2, waiting for transfers between devices, prefix(): everything = jax.tree.map(lambda part: lax.all_gather(part, axis), array)  170 us
    select_n x64, other arithmetic, lap(): return jax.tree.map(lambda a, b: jnp.where(reached, a, b), new, before)  67.6 us
    all_gather x1, blocking collectives, prefix(): everything = jax.tree.map(lambda part: lax.all_gather(part, axis), array)  31.4 us
    psum x1, blocking collectives, shards(): squares, inner_sums = lax.psum((squares, inner_sums), 'tp')  25.1 us
  transfers between devices with their start and end apart: 2, of which 2 were waited for; matrix products, arithmetic and copies ran while one was open for 2% of the time, Pallas kernels for 0%

commit v1 on v0

v1 whole, which is shorter than its diff:
```python
import functools

import jax
import jax.numpy as jnp
from jax import lax
from jax.experimental import pallas as pl
from jax.experimental.pallas import tpu as pltpu
from jax.sharding import PartitionSpec as P

DK = 128
BLOCK = 256
FEATURES = 8192
EPSILON = 1e-06
F32 = jnp.float32
BF16 = jnp.bfloat16


def dot(a, b, ca, cb):
    return lax.dot_general(a, b, (((ca,), (cb,)), ((), ())), preferred_element_type=F32)


def head(ref, h):
    return ref[:, h * DK : (h + 1) * DK]


def thirds(x):
    hi = x.astype(BF16)
    rest = x - hi.astype(F32)
    mid = rest.astype(BF16)
    lo = (rest - mid.astype(F32)).astype(BF16)
    return hi, mid, lo


def triangle():
    row = lax.broadcasted_iota(jnp.int32, (BLOCK, BLOCK), 0)
    col = lax.broadcasted_iota(jnp.int32, (BLOCK, BLOCK), 1)
    return row >= col


def cum_columns(log_decay, low):
    return sum(dot(low, part, 1, 1) for part in thirds(log_decay))


def cum_rows(log_decay, low):
    return sum(dot(part, low, 1, 1) for part in thirds(log_decay))


def update_kernel(k_ref, v_ref, ld_ref, kd_ref, update_ref, fade_ref):
    heads = ld_ref.shape[0]
    low = triangle().astype(F32).astype(BF16)
    cum = cum_columns(ld_ref[...], low)
    total = cum[BLOCK - 1 : BLOCK, :]
    fall = jnp.exp(total - cum)
    fade = jnp.exp(total)
    pieces = update_ref.shape[0] // heads
    for h in range(heads):
        kd = (head(k_ref, h).astype(F32) * fall[:, h : h + 1]).astype(BF16)
        kd_ref[:, h * DK : (h + 1) * DK] = kd
        update = dot(kd, head(v_ref, h), 0, 0)
        update_ref[h * pieces : (h + 1) * pieces] = update.reshape(pieces, -1, DK)
        fade_ref[h * pieces : (h + 1) * pieces] = jnp.broadcast_to(
            fade[:, h : h + 1].reshape(1, 1, 1), (pieces, 1, DK)
        )


def decay_mask(causal, columns, rows, h):
    spread = columns[:, h : h + 1] - rows[h : h + 1, :]
    return jnp.where(causal, jnp.exp(jnp.minimum(spread, 0.0)), 0.0)


def local_kernel(q_ref, k_ref, v_ref, ld_ref, qd_ref, scored_ref, local_ref):
    heads = ld_ref.shape[0]
    causal = triangle()
    low = causal.astype(F32).astype(BF16)
    columns = cum_columns(ld_ref[...], low)
    rows = cum_rows(ld_ref[...], low)
    rise = jnp.exp(columns)
    for h in range(heads):
        q = head(q_ref, h)
        qd_ref[:, h * DK : (h + 1) * DK] = (q.astype(F32) * rise[:, h : h + 1]).astype(BF16)
        scores = dot(q, head(k_ref, h), 1, 1)
        scored = (scores * decay_mask(causal, columns, rows, h)).astype(BF16)
        scored_ref[h] = scored
        local_ref[:, h * DK : (h + 1) * DK] = dot(scored, head(v_ref, h), 1, 0)


def scan_kernel(reverse, fade_ref, update_ref, before_ref):
    size = update_ref.shape[0]
    carried = jnp.zeros(update_ref.shape[1:], F32)
    for step in range(size):
        at = size - 1 - step if reverse else step
        before_ref[at] = carried
        carried = carried * fade_ref[at] + update_ref[at]


def attend_kernel(local_ref, qd_ref, state_ref, gain_ref, dn_ref, att_ref, sums_ref):
    heads = state_ref.shape[0]
    squares = jnp.zeros((BLOCK, DK), F32)
    inner = jnp.zeros((BLOCK, DK), F32)
    for h in range(heads):
        att = head(local_ref, h) + dot(head(qd_ref, h), state_ref[h].astype(BF16), 1, 0)
        att = att.astype(BF16)
        att_ref[:, h * DK : (h + 1) * DK] = att
        wide = att.astype(F32)
        gained = head(gain_ref, h) * head(dn_ref, h).astype(F32)
        squares += wide * wide
        inner += wide * gained
    squares = jnp.sum(jnp.transpose(squares), axis=0, keepdims=True)
    inner = jnp.sum(jnp.transpose(inner), axis=0, keepdims=True)
    mine = jnp.concatenate(
        [squares[:, :DK], squares[:, DK:], inner[:, :DK], inner[:, DK:]], axis=0
    )
    sums_ref[...] = jnp.broadcast_to(mine[None], sums_ref.shape)


def norm_kernel(att_ref, qd_ref, gain_ref, dn_ref, sums_ref, da_ref, update_ref):
    heads = att_ref.shape[1] // DK
    pieces = update_ref.shape[0] // heads
    sums = jnp.sum(sums_ref[...], axis=0)
    squares, inner = sums[0:2], sums[2:4]
    inv_rms = lax.rsqrt(squares * (1.0 / FEATURES) + EPSILON)
    pull = inv_rms * inv_rms * inv_rms * inner * (1.0 / FEATURES)
    scales = jnp.transpose(jnp.concatenate([inv_rms, pull, inv_rms, pull], axis=0))
    inv_rms = jnp.concatenate([scales[:, 0:1], scales[:, 1:2]], axis=0)
    pull = jnp.concatenate([scales[:, 2:3], scales[:, 3:4]], axis=0)
    for h in range(heads):
        gained = head(gain_ref, h) * head(dn_ref, h).astype(F32)
        da = (inv_rms * gained - head(att_ref, h).astype(F32) * pull).astype(BF16)
        da_ref[:, h * DK : (h + 1) * DK] = da
        update = dot(head(qd_ref, h), da, 0, 0)
        update_ref[h * pieces : (h + 1) * pieces] = update.reshape(pieces, -1, DK)


def grads_kernel(
    q_ref, k_ref, v_ref, ld_ref, scored_ref, state_ref, da_ref, dq_ref, dk_ref, dv_ref
):
    heads = ld_ref.shape[0]
    causal = triangle()
    low = causal.astype(F32).astype(BF16)
    columns = cum_columns(ld_ref[...], low)
    rows = cum_rows(ld_ref[...], low)
    rise = jnp.exp(columns)
    for h in range(heads):
        da = head(da_ref, h)
        here = slice(h * DK, (h + 1) * DK)
        d_scores = dot(da, head(v_ref, h), 1, 1)
        d_scored = (d_scores * decay_mask(causal, columns, rows, h)).astype(BF16)
        dq = dot(d_scored, head(k_ref, h), 1, 0)
        dq += rise[:, h : h + 1] * dot(da, state_ref[h].astype(BF16), 1, 1)
        dq_ref[:, here] = dq.astype(BF16)
        dk_ref[:, here] = dot(d_scored, head(q_ref, h), 0, 0)
        dv_ref[:, here] = dot(scored_ref[h], da, 0, 0)


def final_kernel(dk_local_ref, dv_local_ref, v_ref, kd_ref, ld_ref, grad_ref, dk_ref, dv_ref):
    heads = ld_ref.shape[0]
    low = triangle().astype(F32).astype(BF16)
    cum = cum_columns(ld_ref[...], low)
    fall = jnp.exp(cum[BLOCK - 1 : BLOCK, :] - cum)
    for h in range(heads):
        here = slice(h * DK, (h + 1) * DK)
        grad = grad_ref[h].astype(BF16)
        dk = head(dk_local_ref, h) + fall[:, h : h + 1] * dot(head(v_ref, h), grad, 1, 1)
        dk_ref[:, here] = dk.astype(BF16)
        dv = head(dv_local_ref, h) + dot(head(kd_ref, h), grad, 1, 0)
        dv_ref[:, here] = dv.astype(BF16)


def call(kernel, outs, flops, *args):
    moved = sum(a.size * a.dtype.itemsize for a in (*args, *outs))
    return pl.pallas_call(
        kernel,
        out_shape=outs,
        compiler_params=pltpu.CompilerParams(vmem_limit_bytes=32 << 20),
        cost_estimate=pl.CostEstimate(flops=flops, bytes_accessed=moved, transcendentals=0),
    )(*args)


def shape(dims, dtype=F32):
    return jax.ShapeDtypeStruct(dims, dtype)


def exchange(array, axis):
    return lax.all_to_all(array, axis, 0, 0, tiled=True)


def shards(query_rows, key_rows, value_rows, log_decay, norm_gain, d_normed):
    heads = log_decay.shape[0]
    ctx, tp = lax.axis_size("ctx"), lax.axis_size("tp")
    wide = heads * DK
    piece = heads * DK // ctx
    pieces = (ctx, piece, DK)
    rows, square = (BLOCK, wide), (heads, BLOCK, BLOCK)
    unit = 2 * heads * BLOCK * DK * DK
    gain = norm_gain.reshape(1, wide)

    k_decayed, updates, fade = call(
        update_kernel,
        (shape(rows, BF16), shape(pieces), shape((ctx, 1, DK))),
        unit,
        key_rows,
        value_rows,
        log_decay,
    )
    packed = jnp.concatenate([updates, fade], axis=1)[:, :, None, :]
    packed = exchange(packed, "ctx")
    fades = packed[:, piece:, 0, :]
    before = call(
        functools.partial(scan_kernel, False),
        (shape(pieces),),
        unit // 32,
        fades,
        packed[:, :piece, 0, :],
    )[0]
    q_decayed, scored, local = call(
        local_kernel,
        (shape(rows, BF16), shape(square, BF16), shape(rows)),
        6 * unit,
        query_rows,
        key_rows,
        value_rows,
        log_decay,
    )
    states = exchange(before, "ctx").reshape(heads, DK, DK)
    attended, sums = call(
        attend_kernel,
        (shape(rows, BF16), shape((tp, 4, DK))),
        unit,
        local,
        q_decayed,
        states,
        gain,
        d_normed,
    )
    sums = exchange(sums, "tp")
    d_attended, updates = call(
        norm_kernel,
        (shape(rows, BF16), shape(pieces)),
        unit,
        attended,
        q_decayed,
        gain,
        d_normed,
        sums,
    )
    after = call(
        functools.partial(scan_kernel, True),
        (shape(pieces),),
        unit // 32,
        fades,
        exchange(updates, "ctx"),
    )[0]
    d_query, dk_local, dv_local = call(
        grads_kernel,
        (shape(rows, BF16), shape(rows), shape(rows)),
        10 * unit,
        query_rows,
        key_rows,
        value_rows,
        log_decay,
        scored,
        states,
        d_attended,
    )
    grads = exchange(after, "ctx").reshape(heads, DK, DK)
    d_key, d_value = call(
        final_kernel,
        (shape(rows, BF16), shape(rows, BF16)),
        2 * unit,
        dk_local,
        dv_local,
        value_rows,
        k_decayed,
        log_decay,
        grads,
    )
    return d_query, d_key, d_value


def solution(mesh):
    placed = (
        P("ctx", "tp"),
        P("ctx", "tp"),
        P("ctx", "tp"),
        P("tp", "ctx"),
        P("tp"),
        P("ctx", "tp"),
    )
    return jax.shard_map(
        shards,
        mesh=mesh,
        in_specs=placed,
        out_specs=(P("ctx", "tp"), P("ctx", "tp"), P("ctx", "tp")),
        check_vma=False,
    )
```

time: 329 us -> 99.6 us (0.30)
  waiting for transfers between devices: 170 us -> 17.8 us
  other arithmetic: 69.2 us -> 0.03 us
  between operations: 14.2 us -> 0.79 us
  starting transfers between devices: 0.08 us -> 9.35 us
  Pallas kernels: 0 us -> 7.58 us
  matrix products: 7.35 us -> 0 us
    all_gather x2 -> x0, waiting for transfers between devices: 170 us -> none  [prefix(): everything = jax.tree.map(lambda part: lax.all_gather(part, axis), array)]
    select_n x64 -> x0, other arithmetic: 67.6 us -> none  [lap(): return jax.tree.map(lambda a, b: jnp.where(reached, a, b), new, before)]
    all_to_all x0 -> x3, blocking collectives: none -> 58 us  [exchange(): return lax.all_to_all(array, axis, 0, 0, tiled=True)]
    all_gather x1 -> x0, blocking collectives: 31.4 us -> none  [prefix(): everything = jax.tree.map(lambda part: lax.all_gather(part, axis), array)]
    psum x1 -> x0, blocking collectives: 25.1 us -> none  [shards(): squares, inner_sums = lax.psum((squares, inner_sums), 'tp')]
    all_to_all x0 -> x2, waiting for transfers between devices: none -> 17.8 us  [exchange(): return lax.all_to_all(array, axis, 0, 0, tiled=True)]
    all_to_all x0 -> x2, starting transfers between devices: none -> 9.35 us  [exchange(): return lax.all_to_all(array, axis, 0, 0, tiled=True)]
    pallas_call x0 -> x8, Pallas kernels: none -> 7.58 us  [call(): pl.pallas_call(kernel, out_shape=outs, compiler_params=pltpu.CompilerPara...]
  transfers between devices with their start and end apart: 2 -> 2, of which waited for: 2 -> 2; matrix products, arithmetic and copies ran while one was open for 2% -> 0% of each run, Pallas kernels for 0% -> 3%
where the time goes in v1:
time: 99.6 us; the launch traced here: 97.9 us
  blocking collectives  58 us (58%)
  waiting for transfers between devices  17.8 us (18%)
  starting transfers between devices  9.35 us (9%)
  Pallas kernels  7.58 us (8%)
  local copies, waits for them, and re-layouts  4.31 us (4%)
    all_to_all x3, blocking collectives, exchange(): return lax.all_to_all(array, axis, 0, 0, tiled=True)  58 us
    all_to_all x2, waiting for transfers between devices, exchange(): return lax.all_to_all(array, axis, 0, 0, tiled=True)  17.8 us
    all_to_all x2, starting transfers between devices, exchange(): return lax.all_to_all(array, axis, 0, 0, tiled=True)  9.35 us
    pallas_call x8, Pallas kernels, call(): pl.pallas_call(kernel, out_shape=outs, compiler_params=pltpu.CompilerPara...  7.58 us
    unnamed x22, local copies, waits for them, and re-layouts  3.99 us
  transfers between devices with their start and end apart: 2, of which 2 were waited for; matrix products, arithmetic and copies ran while one was open for 0% of the time, Pallas kernels for 3%

profile of v1, /device:TPU:1, one launch (start us, length us, event | category | flops | bytes accessed | tf_op | source)
XLA Modules:
  0.0 97.9 jit_solution(8675952525101121334)
XLA Ops:
  0.6 0.0 copy-start
  0.6 0.9 copy-done
  1.6 0.0 copy-start.2
  1.6 0.9 copy-done.2
  2.5 0.0 copy-start.8
  2.5 0.7 copy-done.8
  3.2 0.8 shard_map.86
  4.0 0.3 copy.12
  4.3 22.1 %all_to_all.25 = f32[32,17,1,128]{3,2,1,0:T(1,128)S(1)} all-to-all(f32[32,17,1,128]{3,2,1,0:T(1,128)S(1)} %copy.12), channel_id=1, replica_groups=mesh['ctx'=32,'tp'=16] {'ctx'}, dimensions={0} | all-to-all | bytes 557056 | tf_op jit(solution)/shard_map/all_to_all | solution.py:184
  26.5 0.0 copy-start.5
  26.5 0.0 copy-start.9
  26.5 0.8 shard_map.87
  27.3 0.0 copy-start.1
  27.3 0.0 copy-start.3
  27.3 4.6 %all-to-all-start.1 = ((f32[32,16,128]{2,1,0:T(8,128)}), f32[32,16,128]{2,1,0:T(8,128)S(1)}, u32[]{:S(2)}, u32[]{:S(2)}) async-start(f32[32,16,128]{2,1,0:T(8,128)} %shard_map.87), calls=%async_computation.1 | async-start | bytes 524288 | tf_op jit(solution)/shard_map/all_to_all | solution.py:184
  31.9 0.0 copy-done.5
  31.9 0.0 copy-done.9
  31.9 0.0 copy-done.1
  31.9 0.0 copy-done.3
  31.9 0.0 copy-start.4
  31.9 0.8 shard_map.85
  32.7 9.6 %all-to-all-done.1 = f32[32,16,128]{2,1,0:T(8,128)S(1)} async-done(((f32[32,16,128]{2,1,0:T(8,128)}), f32[32,16,128]{2,1,0:T(8,128)S(1)}, u32[]{:S(2)}, u32[]{:S(2)}) %all-to-all-start.1) | async-done | bytes 262176 | tf_op jit(solution)/shard_map/all_to_all | solution.py:184
  42.3 0.0 copy-start.10
  42.3 0.0 copy-done.4
  42.3 0.7 copy-done.10
  43.0 0.4 shard_map.88
  43.4 21.3 %all_to_all.26.sums_ref = f32[16,4,128]{2,1,0:T(4,128)S(1)} all-to-all(f32[16,4,128]{2,1,0:T(4,128)S(1)} %get-tuple-element.24), channel_id=1, replica_groups=mesh['ctx'=32,'tp'=16] {'tp'}, dimensions={0} | all-to-all | bytes 65536 | tf_op jit(solution)/shard_map/all_to_all | solution.py:184
  64.6 0.5 shard_map.89
  65.2 0.0 copy-start.6
  65.2 0.7 copy-done.6
  65.9 14.6 %all_to_all.27.update_ref = f32[32,16,128]{2,1,0:T(8,128)S(1)} all-to-all(f32[32,16,128]{2,1,0:T(8,128)S(1)} %get-tuple-element.30), channel_id=1, replica_groups=mesh['ctx'=32,'tp'=16] {'ctx'}, dimensions={0} | all-to-all | bytes 524288 | tf_op jit(solution)/shard_map/all_to_all | solution.py:184
  80.5 0.8 shard_map.91
  81.3 0.0 copy-start.7
  81.3 4.8 %all-to-all-start.4 = ((f32[32,16,128]{2,1,0:T(8,128)}), f32[32,16,128]{2,1,0:T(8,128)S(1)}, u32[]{:S(2)}, u32[]{:S(2)}) async-start(f32[32,16,128]{2,1,0:T(8,128)} %shard_map.91), calls=%async_computation.4 | async-start | bytes 524288 | tf_op jit(solution)/shard_map/all_to_all | solution.py:184
  86.1 0.0 copy-done.7
  86.1 2.3 %shard_map.90 = (bf16[256,512]{1,0:T(8,128)(2,1)}, f32[256,512]{1,0:T(8,128)S(1)}, f32[256,512]{1,0:T(8,128)S(1)}) custom-call(bf16[256,512]{1,0:T(8,128)(2,1)S(1)} %copy-done.5, bf16[256,512]{1,0:T(8,128)(2,1)S(1)} %copy-done.3, bf16[256,512]{1,0:T(8,128)(2,1)S(1)} %copy-done.1, f32[4,256]{1,0:T(4,128)S(1)} %copy-done.9, ...), custom_call_target="tpu_custom_call" | custom-call | flops 335544320 | bytes 3149824 | tf_op jit(solution)/shard_map/pallas_call | solution.py:171
  88.3 8.2 %all-to-all-done.4 = f32[32,16,128]{2,1,0:T(8,128)S(1)} async-done(((f32[32,16,128]{2,1,0:T(8,128)}), f32[32,16,128]{2,1,0:T(8,128)S(1)}, u32[]{:S(2)}, u32[]{:S(2)}) %all-to-all-start.4) | async-done | bytes 262176 | tf_op jit(solution)/shard_map/all_to_all | solution.py:184
  96.6 1.3 %shard_map.92 = (bf16[256,512]{1,0:T(8,128)(2,1)}, bf16[256,512]{1,0:T(8,128)(2,1)}) custom-call(f32[256,512]{1,0:T(8,128)S(1)} %get-tuple-element.27.dk_local_ref, f32[256,512]{1,0:T(8,128)S(1)} %get-tuple-element.28.dv_local_ref, bf16[256,512]{1,0:T(8,128)(2,1)S(1)} %copy-done.1, bf16[256,512]{1,0:T(8,128)(2,1)S(1)} %get-tuple-element.29.kd_ref, ...), custom_call_target="tpu_custom_call" | custom-call | flops 67108864 | bytes 2363392 | tf_op jit(solution)/shard_map/pallas_call | solution.py:171
  (3 shorter events, 0.1 us)
Async XLA Ops:
  0.6 1.0 copy-start
  1.6 0.9 copy-start.2
  2.5 0.7 copy-start.8
  26.5 5.4 %copy-start.5 = (bf16[256,512]{1,0:T(8,128)(2,1)S(1)}, bf16[256,512]{1,0:T(8,128)(2,1)}, u32[]{:S(2)}) copy-start(bf16[256,512]{1,0:T(8,128)(2,1)} %q_ref.3) | copy-start | bytes 786436
  26.5 5.4 %copy-start.9 = (f32[4,256]{1,0:T(4,128)S(1)}, f32[4,256]{1,0:T(4,128)}, u32[]{:S(2)}) copy-start(f32[4,256]{1,0:T(4,128)} %ld_ref.7) | copy-start | bytes 12292
  27.3 4.6 %copy-start.1 = (bf16[256,512]{1,0:T(8,128)(2,1)S(1)}, bf16[256,512]{1,0:T(8,128)(2,1)}, u32[]{:S(2)}) copy-start(bf16[256,512]{1,0:T(8,128)(2,1)} %v_ref.7) | copy-start | bytes 786436
  27.3 4.6 %copy-start.3 = (bf16[256,512]{1,0:T(8,128)(2,1)S(1)}, bf16[256,512]{1,0:T(8,128)(2,1)}, u32[]{:S(2)}) copy-start(bf16[256,512]{1,0:T(8,128)(2,1)} %k_ref.5) | copy-start | bytes 786436
  27.3 15.0 %all-to-all-start.1 = ((f32[32,16,128]{2,1,0:T(8,128)}), f32[32,16,128]{2,1,0:T(8,128)S(1)}, u32[]{:S(2)}, u32[]{:S(2)}) async-start(f32[32,16,128]{2,1,0:T(8,128)} %shard_map.87), calls=%async_computation.1 | async-start | bytes 524288 | tf_op jit(solution)/shard_map/all_to_all | solution.py:184
  31.9 10.4 %copy-start.4 = (bf16[256,512]{1,0:T(8,128)(2,1)S(1)}, bf16[256,512]{1,0:T(8,128)(2,1)}, u32[]{:S(2)}) copy-start(bf16[256,512]{1,0:T(8,128)(2,1)} %dn_ref.3) | copy-start | bytes 786436
  42.3 0.7 copy-start.10
  65.2 0.7 copy-start.6
  81.3 4.8 %copy-start.7 = (bf16[256,512]{1,0:T(8,128)(2,1)S(1)}, bf16[256,512]{1,0:T(8,128)(2,1)}, u32[]{:S(2)}) copy-start(bf16[256,512]{1,0:T(8,128)(2,1)} %copy-done.6) | copy-start | bytes 786436
  81.3 15.3 %all-to-all-start.4 = ((f32[32,16,128]{2,1,0:T(8,128)}), f32[32,16,128]{2,1,0:T(8,128)S(1)}, u32[]{:S(2)}, u32[]{:S(2)}) async-start(f32[32,16,128]{2,1,0:T(8,128)} %shard_map.91), calls=%async_computation.4 | async-start | bytes 524288 | tf_op jit(solution)/shard_map/all_to_all | solution.py:184

commit v2 on v1

--- a/solution.py
+++ b/solution.py
@@ -45,21 +45,33 @@
     return sum(dot(part, low, 1, 1) for part in thirds(log_decay))
 
 
-def update_kernel(k_ref, v_ref, ld_ref, kd_ref, update_ref, fade_ref):
+def update_kernel(k_hbm, v_hbm, ld_hbm, kd_ref, packed_ref, k_ref, v_ref, ld_ref, sems):
     heads = ld_ref.shape[0]
+    copies = [pltpu.make_async_copy(ld_hbm, ld_ref, sems.at[2 * heads])]
+    for h in range(heads):
+        here = (slice(None), slice(h * DK, (h + 1) * DK))
+        copies.append(pltpu.make_async_copy(k_hbm.at[here], k_ref.at[here], sems.at[2 * h]))
+        copies.append(pltpu.make_async_copy(v_hbm.at[here], v_ref.at[here], sems.at[2 * h + 1]))
+    for copy in copies:
+        copy.start()
     low = triangle().astype(F32).astype(BF16)
+    copies[0].wait()
     cum = cum_columns(ld_ref[...], low)
     total = cum[BLOCK - 1 : BLOCK, :]
     fall = jnp.exp(total - cum)
     fade = jnp.exp(total)
-    pieces = update_ref.shape[0] // heads
-    for h in range(heads):
+    pieces = packed_ref.shape[0] // heads
+    piece = DK // pieces
+    for h in range(heads):
+        these = slice(h * pieces, (h + 1) * pieces)
+        copies[2 * h + 1].wait()
         kd = (head(k_ref, h).astype(F32) * fall[:, h : h + 1]).astype(BF16)
         kd_ref[:, h * DK : (h + 1) * DK] = kd
+        copies[2 * h + 2].wait()
         update = dot(kd, head(v_ref, h), 0, 0)
-        update_ref[h * pieces : (h + 1) * pieces] = update.reshape(pieces, -1, DK)
-        fade_ref[h * pieces : (h + 1) * pieces] = jnp.broadcast_to(
-            fade[:, h : h + 1].reshape(1, 1, 1), (pieces, 1, DK)
+        packed_ref[these, 0:piece] = update.reshape(pieces, piece, 1, DK)
+        packed_ref[these, piece : piece + 1] = jnp.broadcast_to(
+            fade[:, h : h + 1].reshape(1, 1, 1, 1), (pieces, 1, 1, DK)
         )
 
 
@@ -68,7 +80,10 @@
     return jnp.where(causal, jnp.exp(jnp.minimum(spread, 0.0)), 0.0)
 
 
-def local_kernel(q_ref, k_ref, v_ref, ld_ref, qd_ref, scored_ref, local_ref):
+def local_kernel(
+    q_ref, k_ref, v_ref, ld_ref, gain_ref, dn_ref, qd_ref, scored_ref, local_ref, gained_ref
+):
+    gained_ref[...] = gain_ref[...] * dn_ref[...].astype(F32)
     heads = ld_ref.shape[0]
     causal = triangle()
     low = causal.astype(F32).astype(BF16)
@@ -93,7 +108,7 @@
         carried = carried * fade_ref[at] + update_ref[at]
 
 
-def attend_kernel(local_ref, qd_ref, state_ref, gain_ref, dn_ref, att_ref, sums_ref):
+def attend_kernel(local_ref, qd_ref, state_ref, gained_ref, att_ref, sums_ref):
     heads = state_ref.shape[0]
     squares = jnp.zeros((BLOCK, DK), F32)
     inner = jnp.zeros((BLOCK, DK), F32)
@@ -102,9 +117,8 @@
         att = att.astype(BF16)
         att_ref[:, h * DK : (h + 1) * DK] = att
         wide = att.astype(F32)
-        gained = head(gain_ref, h) * head(dn_ref, h).astype(F32)
         squares += wide * wide
-        inner += wide * gained
+        inner += wide * head(gained_ref, h)
     squares = jnp.sum(jnp.transpose(squares), axis=0, keepdims=True)
     inner = jnp.sum(jnp.transpose(inner), axis=0, keepdims=True)
     mine = jnp.concatenate(
@@ -113,7 +127,7 @@
     sums_ref[...] = jnp.broadcast_to(mine[None], sums_ref.shape)
 
 
-def norm_kernel(att_ref, qd_ref, gain_ref, dn_ref, sums_ref, da_ref, update_ref):
+def norm_kernel(att_ref, qd_ref, gained_ref, sums_ref, da_ref, update_ref):
     heads = att_ref.shape[1] // DK
     pieces = update_ref.shape[0] // heads
     sums = jnp.sum(sums_ref[...], axis=0)
@@ -124,8 +138,8 @@
     inv_rms = jnp.concatenate([scales[:, 0:1], scales[:, 1:2]], axis=0)
     pull = jnp.concatenate([scales[:, 2:3], scales[:, 3:4]], axis=0)
     for h in range(heads):
-        gained = head(gain_ref, h) * head(dn_ref, h).astype(F32)
-        da = (inv_rms * gained - head(att_ref, h).astype(F32) * pull).astype(BF16)
+        da = inv_rms * head(gained_ref, h) - head(att_ref, h).astype(F32) * pull
+        da = da.astype(BF16)
         da_ref[:, h * DK : (h + 1) * DK] = da
         update = dot(head(qd_ref, h), da, 0, 0)
         update_ref[h * pieces : (h + 1) * pieces] = update.reshape(pieces, -1, DK)
@@ -152,28 +166,41 @@
         dv_ref[:, here] = dot(scored_ref[h], da, 0, 0)
 
 
-def final_kernel(dk_local_ref, dv_local_ref, v_ref, kd_ref, ld_ref, grad_ref, dk_ref, dv_ref):
+def final_kernel(
+    dk_local_ref, dv_local_ref, v_ref, kd_ref, ld_ref, grad_ref, dk_hbm, dv_hbm, dk_ref, dv_ref, sems
+):
     heads = ld_ref.shape[0]
     low = triangle().astype(F32).astype(BF16)
     cum = cum_columns(ld_ref[...], low)
     fall = jnp.exp(cum[BLOCK - 1 : BLOCK, :] - cum)
-    for h in range(heads):
-        here = slice(h * DK, (h + 1) * DK)
+    copies = []
+    for h in range(heads):
+        here = (slice(None), slice(h * DK, (h + 1) * DK))
         grad = grad_ref[h].astype(BF16)
         dk = head(dk_local_ref, h) + fall[:, h : h + 1] * dot(head(v_ref, h), grad, 1, 1)
-        dk_ref[:, here] = dk.astype(BF16)
+        dk_ref[here] = dk.astype(BF16)
         dv = head(dv_local_ref, h) + dot(head(kd_ref, h), grad, 1, 0)
-        dv_ref[:, here] = dv.astype(BF16)
-
-
-def call(kernel, outs, flops, *args):
+        dv_ref[here] = dv.astype(BF16)
+        copies.append(pltpu.make_async_copy(dk_ref.at[here], dk_hbm.at[here], sems.at[2 * h]))
+        copies.append(pltpu.make_async_copy(dv_ref.at[here], dv_hbm.at[here], sems.at[2 * h + 1]))
+        copies[-2].start()
+        copies[-1].start()
+    for copy in copies:
+        copy.wait()
+
+
+def call(kernel, outs, flops, *args, **kinds):
     moved = sum(a.size * a.dtype.itemsize for a in (*args, *outs))
     return pl.pallas_call(
         kernel,
         out_shape=outs,
-        compiler_params=pltpu.CompilerParams(vmem_limit_bytes=32 << 20),
+        compiler_params=pltpu.CompilerParams(vmem_limit_bytes=8 << 20),
         cost_estimate=pl.CostEstimate(flops=flops, bytes_accessed=moved, transcendentals=0),
+        **kinds,
     )(*args)
+
+
+IN_HBM = pl.BlockSpec(memory_space=pltpu.HBM)
 
 
 def shape(dims, dtype=F32):
@@ -194,15 +221,19 @@
     unit = 2 * heads * BLOCK * DK * DK
     gain = norm_gain.reshape(1, wide)
 
-    k_decayed, updates, fade = call(
+    k_decayed, packed = call(
         update_kernel,
-        (shape(rows, BF16), shape(pieces), shape((ctx, 1, DK))),
+        (shape(rows, BF16), shape((ctx, piece + 1, 1, DK))),
         unit,
-        key_rows,
-        value_rows,
-        log_decay,
-    )
-    packed = jnp.concatenate([updates, fade], axis=1)[:, :, None, :]
+        *(pltpu.with_memory_space_constraint(x, pltpu.HBM) for x in (key_rows, value_rows, log_decay)),
+        in_specs=[IN_HBM] * 3,
+        scratch_shapes=[
+            pltpu.VMEM(rows, BF16),
+            pltpu.VMEM(rows, BF16),
+            pltpu.VMEM(log_decay.shape, F32),
+            pltpu.SemaphoreType.DMA((2 * heads + 1,)),
+        ],
+    )
     packed = exchange(packed, "ctx")
     fades = packed[:, piece:, 0, :]
     before = call(
@@ -212,14 +243,16 @@
         fades,
         packed[:, :piece, 0, :],
     )[0]
-    q_decayed, scored, local = call(
+    q_decayed, scored, local, gained = call(
         local_kernel,
-        (shape(rows, BF16), shape(square, BF16), shape(rows)),
+        (shape(rows, BF16), shape(square, BF16), shape(rows), shape(rows)),
         6 * unit,
         query_rows,
         key_rows,
         value_rows,
         log_decay,
+        gain,
+        d_normed,
     )
     states = exchange(before, "ctx").reshape(heads, DK, DK)
     attended, sums = call(
@@ -229,8 +262,7 @@
         local,
         q_decayed,
         states,
-        gain,
-        d_normed,
+        gained,
     )
     sums = exchange(sums, "tp")
     d_attended, updates = call(
@@ -239,8 +271,7 @@
         unit,
         attended,
         q_decayed,
-        gain,
-        d_normed,
+        gained,
         sums,
     )
     after = call(
@@ -273,6 +304,12 @@
         k_decayed,
         log_decay,
         grads,
+        out_specs=(IN_HBM, IN_HBM),
+        scratch_shapes=[
+            pltpu.VMEM(rows, BF16),
+            pltpu.VMEM(rows, BF16),
+            pltpu.SemaphoreType.DMA((2 * heads,)),
+        ],
     )
     return d_query, d_key, d_value
 

time: 99.6 us -> 97.5 us (0.979)
  local copies, waits for them, and re-layouts: 4.31 us -> 0.78 us
  Pallas kernels: 7.58 us -> 9.2 us
    unnamed x22 -> x20, local copies, waits for them, and re-layouts: 3.99 us -> 0.75 us
    pallas_call x8, Pallas kernels: 7.58 us -> 9.2 us  [call(): pl.pallas_call(kernel, out_shape=outs, compiler_params=pltpu.CompilerPara...]
where the time goes in v2:
time: 97.5 us; the launch traced here: 95.9 us
  blocking collectives  58 us (59%)
  waiting for transfers between devices  17.7 us (18%)
  starting transfers between devices  9.35 us (10%)
  Pallas kernels  9.2 us (9%)
    all_to_all x3, blocking collectives, exchange(): return lax.all_to_all(array, axis, 0, 0, tiled=True)  58 us
    all_to_all x2, waiting for transfers between devices, exchange(): return lax.all_to_all(array, axis, 0, 0, tiled=True)  17.7 us
    all_to_all x2, starting transfers between devices, exchange(): return lax.all_to_all(array, axis, 0, 0, tiled=True)  9.35 us
    pallas_call x8, Pallas kernels, call(): pl.pallas_call(kernel, out_shape=outs, compiler_params=pltpu.CompilerPara...  9.2 us
  transfers between devices with their start and end apart: 2, of which 2 were waited for; matrix products, arithmetic and copies ran while one was open for 0% of the time, Pallas kernels for 3%

profile of v2, /device:TPU:1, one launch (start us, length us, event | category | flops | bytes accessed | tf_op | source)
XLA Modules:
  0.0 95.9 jit_solution(2840966013586797818)
XLA Ops:
  0.6 2.4 %shard_map.86 = (bf16[256,512]{1,0:T(8,128)(2,1)S(1)}, f32[32,17,1,128]{3,2,1,0:T(1,128)S(1)}) custom-call(bf16[256,512]{1,0:T(8,128)(2,1)} %k_ref.3, bf16[256,512]{1,0:T(8,128)(2,1)} %v_ref.5, f32[4,256]{1,0:T(4,128)} %ld_ref.5), custom_call_target="tpu_custom_call" | custom-call | flops 33554432 | bytes 1069056 | tf_op jit(solution)/shard_map/pallas_call | solution.py:194
  3.0 0.0 copy-start.3
  3.0 0.7 copy-done.3
  3.7 22.1 %all_to_all.25 = f32[32,17,1,128]{3,2,1,0:T(1,128)S(1)} all-to-all(f32[32,17,1,128]{3,2,1,0:T(1,128)S(1)} %get-tuple-element.19), channel_id=1, replica_groups=mesh['ctx'=32,'tp'=16] {'ctx'}, dimensions={0} | all-to-all | bytes 557056 | tf_op jit(solution)/shard_map/all_to_all | solution.py:211
  25.8 0.0 copy-start.2
  25.9 0.0 copy-start.7
  25.9 0.0 copy-start.8
  25.9 0.0 copy-start.9
  25.9 0.8 shard_map.87
  26.7 0.0 copy-start
  26.7 0.0 copy-start.1
  26.7 4.6 %all-to-all-start.1 = ((f32[32,16,128]{2,1,0:T(8,128)}), f32[32,16,128]{2,1,0:T(8,128)S(1)}, u32[]{:S(2)}, u32[]{:S(2)}) async-start(f32[32,16,128]{2,1,0:T(8,128)} %shard_map.87), calls=%async_computation.1 | async-start | bytes 524288 | tf_op jit(solution)/shard_map/all_to_all | solution.py:211
  31.3 0.0 copy-done.2
  31.3 0.0 copy-done.7
  31.3 0.0 copy-done.8
  31.3 0.0 copy-done.9
  31.3 0.0 copy-done
  31.3 0.0 copy-done.1
  31.3 0.8 shard_map.85
  32.2 9.5 %all-to-all-done.1 = f32[32,16,128]{2,1,0:T(8,128)S(1)} async-done(((f32[32,16,128]{2,1,0:T(8,128)}), f32[32,16,128]{2,1,0:T(8,128)S(1)}, u32[]{:S(2)}, u32[]{:S(2)}) %all-to-all-start.1) | async-done | bytes 262176 | tf_op jit(solution)/shard_map/all_to_all | solution.py:211
  41.7 0.4 shard_map.88
  42.1 21.3 %all_to_all.26.sums_ref = f32[16,4,128]{2,1,0:T(4,128)S(1)} all-to-all(f32[16,4,128]{2,1,0:T(4,128)S(1)} %get-tuple-element.24), channel_id=1, replica_groups=mesh['ctx'=32,'tp'=16] {'tp'}, dimensions={0} | all-to-all | bytes 65536 | tf_op jit(solution)/shard_map/all_to_all | solution.py:211
  63.3 0.5 shard_map.89
  63.9 0.0 copy-start.5
  63.9 14.6 %all_to_all.27.update_ref = f32[32,16,128]{2,1,0:T(8,128)S(1)} all-to-all(f32[32,16,128]{2,1,0:T(8,128)S(1)} %get-tuple-element.30), channel_id=1, replica_groups=mesh['ctx'=32,'tp'=16] {'ctx'}, dimensions={0} | all-to-all | bytes 524288 | tf_op jit(solution)/shard_map/all_to_all | solution.py:211
  78.5 0.0 copy-done.5
  78.5 0.8 shard_map.91
  79.3 0.0 copy-start.6
  79.3 4.8 %all-to-all-start.4 = ((f32[32,16,128]{2,1,0:T(8,128)}), f32[32,16,128]{2,1,0:T(8,128)S(1)}, u32[]{:S(2)}, u32[]{:S(2)}) async-start(f32[32,16,128]{2,1,0:T(8,128)} %shard_map.91), calls=%async_computation.4 | async-start | bytes 524288 | tf_op jit(solution)/shard_map/all_to_all | solution.py:211
  84.0 0.0 copy-done.6
  84.1 0.0 copy-start.4
  84.1 2.3 %shard_map.90 = (bf16[256,512]{1,0:T(8,128)(2,1)}, f32[256,512]{1,0:T(8,128)S(1)}, f32[256,512]{1,0:T(8,128)S(1)}) custom-call(bf16[256,512]{1,0:T(8,128)(2,1)S(1)} %copy-done.2, bf16[256,512]{1,0:T(8,128)(2,1)S(1)} %copy-done.1, bf16[256,512]{1,0:T(8,128)(2,1)S(1)} %copy-done, f32[4,256]{1,0:T(4,128)S(1)} %copy-done.8, ...), custom_call_target="tpu_custom_call" | custom-call | flops 335544320 | bytes 3149824 | tf_op jit(solution)/shard_map/pallas_call | solution.py:194
  86.3 8.2 %all-to-all-done.4 = f32[32,16,128]{2,1,0:T(8,128)S(1)} async-done(((f32[32,16,128]{2,1,0:T(8,128)}), f32[32,16,128]{2,1,0:T(8,128)S(1)}, u32[]{:S(2)}, u32[]{:S(2)}) %all-to-all-start.4) | async-done | bytes 262176 | tf_op jit(solution)/shard_map/all_to_all | solution.py:211
  94.6 0.0 copy-done.4
  94.6 1.3 %shard_map.92 = (bf16[256,512]{1,0:T(8,128)(2,1)}, bf16[256,512]{1,0:T(8,128)(2,1)}) custom-call(f32[256,512]{1,0:T(8,128)S(1)} %get-tuple-element.27.dk_local_ref, f32[256,512]{1,0:T(8,128)S(1)} %get-tuple-element.28.dv_local_ref, bf16[256,512]{1,0:T(8,128)(2,1)S(1)} %copy-done, bf16[256,512]{1,0:T(8,128)(2,1)S(1)} %copy-done.4, f32[4,256]{1,0:T(4,128)S(1)} %copy-done.8, ...), custom_call_target="tpu_custom_call" | custom-call | flops 67108864 | bytes 2363392 | tf_op jit(solution)/shard_map/pallas_call | solution.py:194
  (2 shorter events, 0.0 us)
Async XLA Ops:
  3.0 0.7 copy-start.3
  25.8 5.4 %copy-start.2 = (bf16[256,512]{1,0:T(8,128)(2,1)S(1)}, bf16[256,512]{1,0:T(8,128)(2,1)}, u32[]{:S(2)}) copy-start(bf16[256,512]{1,0:T(8,128)(2,1)} %q_ref.3) | copy-start | bytes 786436
  25.9 5.4 %copy-start.7 = (bf16[256,512]{1,0:T(8,128)(2,1)S(1)}, bf16[256,512]{1,0:T(8,128)(2,1)}, u32[]{:S(2)}) copy-start(bf16[256,512]{1,0:T(8,128)(2,1)} %dn_ref.1) | copy-start | bytes 786436
  25.9 5.4 %copy-start.8 = (f32[4,256]{1,0:T(4,128)S(1)}, f32[4,256]{1,0:T(4,128)}, u32[]{:S(2)}) copy-start(f32[4,256]{1,0:T(4,128)} %ld_ref.5) | copy-start | bytes 12292
  25.9 5.4 %copy-start.9 = (f32[512]{0:T(512)S(1)}, f32[512]{0:T(512)}, u32[]{:S(2)}) copy-start(f32[512]{0:T(512)} %param.10) | copy-start | bytes 6148
  26.7 4.6 %copy-start = (bf16[256,512]{1,0:T(8,128)(2,1)S(1)}, bf16[256,512]{1,0:T(8,128)(2,1)}, u32[]{:S(2)}) copy-start(bf16[256,512]{1,0:T(8,128)(2,1)} %v_ref.5) | copy-start | bytes 786436
  26.7 4.7 %copy-start.1 = (bf16[256,512]{1,0:T(8,128)(2,1)S(1)}, bf16[256,512]{1,0:T(8,128)(2,1)}, u32[]{:S(2)}) copy-start(bf16[256,512]{1,0:T(8,128)(2,1)} %k_ref.3) | copy-start | bytes 786436
  26.7 15.0 %all-to-all-start.1 = ((f32[32,16,128]{2,1,0:T(8,128)}), f32[32,16,128]{2,1,0:T(8,128)S(1)}, u32[]{:S(2)}, u32[]{:S(2)}) async-start(f32[32,16,128]{2,1,0:T(8,128)} %shard_map.87), calls=%async_computation.1 | async-start | bytes 524288 | tf_op jit(solution)/shard_map/all_to_all | solution.py:211
  63.9 14.7 %copy-start.5 = (bf16[256,512]{1,0:T(8,128)(2,1)}, bf16[256,512]{1,0:T(8,128)(2,1)S(1)}, u32[]{:S(2)}) copy-start(bf16[256,512]{1,0:T(8,128)(2,1)S(1)} %get-tuple-element.25.da_ref) | copy-start | bytes 786436
  79.3 4.8 %copy-start.6 = (bf16[256,512]{1,0:T(8,128)(2,1)S(1)}, bf16[256,512]{1,0:T(8,128)(2,1)}, u32[]{:S(2)}) copy-start(bf16[256,512]{1,0:T(8,128)(2,1)} %copy-done.5) | copy-start | bytes 786436
  79.3 15.3 %all-to-all-start.4 = ((f32[32,16,128]{2,1,0:T(8,128)}), f32[32,16,128]{2,1,0:T(8,128)S(1)}, u32[]{:S(2)}, u32[]{:S(2)}) async-start(f32[32,16,128]{2,1,0:T(8,128)} %shard_map.91), calls=%async_computation.4 | async-start | bytes 524288 | tf_op jit(solution)/shard_map/all_to_all | solution.py:211
  84.1 10.5 %copy-start.4 = (bf16[256,512]{1,0:T(8,128)(2,1)S(1)}, bf16[256,512]{1,0:T(8,128)(2,1)}, u32[]{:S(2)}) copy-start(bf16[256,512]{1,0:T(8,128)(2,1)} %copy-done.3) | copy-start | bytes 786436

commit v3 on v2

--- a/solution.py
+++ b/solution.py
@@ -1,4 +1,5 @@
 import functools
+import math
 
 import jax
 import jax.numpy as jnp
@@ -45,33 +46,32 @@
     return sum(dot(part, low, 1, 1) for part in thirds(log_decay))
 
 
-def update_kernel(k_hbm, v_hbm, ld_hbm, kd_ref, packed_ref, k_ref, v_ref, ld_ref, sems):
+def update_kernel(k_hbm, v_hbm, ld_hbm, packed_ref, k_ref, v_ref, ld_ref, sems):
     heads = ld_ref.shape[0]
-    copies = [pltpu.make_async_copy(ld_hbm, ld_ref, sems.at[2 * heads])]
-    for h in range(heads):
-        here = (slice(None), slice(h * DK, (h + 1) * DK))
-        copies.append(pltpu.make_async_copy(k_hbm.at[here], k_ref.at[here], sems.at[2 * h]))
-        copies.append(pltpu.make_async_copy(v_hbm.at[here], v_ref.at[here], sems.at[2 * h + 1]))
+    pairs = ((ld_hbm, ld_ref), (k_hbm, k_ref), (v_hbm, v_ref))
+    copies = [pltpu.make_async_copy(*pair, sems.at[i]) for i, pair in enumerate(pairs)]
     for copy in copies:
         copy.start()
     low = triangle().astype(F32).astype(BF16)
     copies[0].wait()
-    cum = cum_columns(ld_ref[...], low)
-    total = cum[BLOCK - 1 : BLOCK, :]
+    cum = cum_rows(ld_ref[...], low)
+    total = cum[:, BLOCK - 1 : BLOCK]
     fall = jnp.exp(total - cum)
     fade = jnp.exp(total)
     pieces = packed_ref.shape[0] // heads
     piece = DK // pieces
+    copies[1].wait()
+    kd = []
+    for h in range(heads):
+        flipped = jnp.transpose(head(k_ref, h)).astype(F32)
+        kd.append((flipped * fall[h : h + 1, :]).astype(BF16))
+    copies[2].wait()
     for h in range(heads):
         these = slice(h * pieces, (h + 1) * pieces)
-        copies[2 * h + 1].wait()
-        kd = (head(k_ref, h).astype(F32) * fall[:, h : h + 1]).astype(BF16)
-        kd_ref[:, h * DK : (h + 1) * DK] = kd
-        copies[2 * h + 2].wait()
-        update = dot(kd, head(v_ref, h), 0, 0)
+        update = dot(kd[h], head(v_ref, h), 1, 0)
         packed_ref[these, 0:piece] = update.reshape(pieces, piece, 1, DK)
         packed_ref[these, piece : piece + 1] = jnp.broadcast_to(
-            fade[:, h : h + 1].reshape(1, 1, 1, 1), (pieces, 1, 1, DK)
+            fade[h : h + 1, :].reshape(1, 1, 1, 1), (pieces, 1, 1, DK)
         )
 
 
@@ -81,22 +81,23 @@
 
 
 def local_kernel(
-    q_ref, k_ref, v_ref, ld_ref, gain_ref, dn_ref, qd_ref, scored_ref, local_ref, gained_ref
+    q_ref, k_ref, v_ref, ld_ref, gain_ref, dn_ref, qd_ref, flipped_ref, local_ref, gained_ref
 ):
+    heads = ld_ref.shape[0]
     gained_ref[...] = gain_ref[...] * dn_ref[...].astype(F32)
-    heads = ld_ref.shape[0]
     causal = triangle()
     low = causal.astype(F32).astype(BF16)
     columns = cum_columns(ld_ref[...], low)
     rows = cum_rows(ld_ref[...], low)
     rise = jnp.exp(columns)
     for h in range(heads):
+        here = slice(h * DK, (h + 1) * DK)
         q = head(q_ref, h)
-        qd_ref[:, h * DK : (h + 1) * DK] = (q.astype(F32) * rise[:, h : h + 1]).astype(BF16)
-        scores = dot(q, head(k_ref, h), 1, 1)
-        scored = (scores * decay_mask(causal, columns, rows, h)).astype(BF16)
-        scored_ref[h] = scored
-        local_ref[:, h * DK : (h + 1) * DK] = dot(scored, head(v_ref, h), 1, 0)
+        qd = (q.astype(F32) * rise[:, h : h + 1]).astype(BF16)
+        qd_ref[:, here] = qd
+        flipped_ref[h] = jnp.transpose(qd)
+        scored = dot(q, head(k_ref, h), 1, 1) * decay_mask(causal, columns, rows, h)
+        local_ref[:, here] = dot(scored.astype(BF16), head(v_ref, h), 1, 0)
 
 
 def scan_kernel(reverse, fade_ref, update_ref, before_ref):
@@ -127,7 +128,7 @@
     sums_ref[...] = jnp.broadcast_to(mine[None], sums_ref.shape)
 
 
-def norm_kernel(att_ref, qd_ref, gained_ref, sums_ref, da_ref, update_ref):
+def norm_kernel(att_ref, flipped_ref, gained_ref, sums_ref, da_ref, update_ref):
     heads = att_ref.shape[1] // DK
     pieces = update_ref.shape[0] // heads
     sums = jnp.sum(sums_ref[...], axis=0)
@@ -141,12 +142,12 @@
         da = inv_rms * head(gained_ref, h) - head(att_ref, h).astype(F32) * pull
         da = da.astype(BF16)
         da_ref[:, h * DK : (h + 1) * DK] = da
-        update = dot(head(qd_ref, h), da, 0, 0)
+        update = dot(flipped_ref[h], da, 1, 0)
         update_ref[h * pieces : (h + 1) * pieces] = update.reshape(pieces, -1, DK)
 
 
 def grads_kernel(
-    q_ref, k_ref, v_ref, ld_ref, scored_ref, state_ref, da_ref, dq_ref, dk_ref, dv_ref
+    q_ref, k_ref, v_ref, ld_ref, state_ref, da_ref, dq_ref, kd_ref, fall_ref, dk_ref, dv_ref
 ):
     heads = ld_ref.shape[0]
     causal = triangle()
@@ -154,30 +155,32 @@
     columns = cum_columns(ld_ref[...], low)
     rows = cum_rows(ld_ref[...], low)
     rise = jnp.exp(columns)
-    for h in range(heads):
-        da = head(da_ref, h)
+    fall = jnp.exp(columns[BLOCK - 1 : BLOCK, :] - columns)
+    for h in range(heads):
         here = slice(h * DK, (h + 1) * DK)
-        d_scores = dot(da, head(v_ref, h), 1, 1)
-        d_scored = (d_scores * decay_mask(causal, columns, rows, h)).astype(BF16)
-        dq = dot(d_scored, head(k_ref, h), 1, 0)
+        q, k, da = head(q_ref, h), head(k_ref, h), head(da_ref, h)
+        fall_wide = jnp.broadcast_to(fall[:, h : h + 1], (BLOCK, DK))
+        fall_ref[:, here] = fall_wide
+        kd_ref[:, here] = (k.astype(F32) * fall_wide).astype(BF16)
+        mask = decay_mask(causal, columns, rows, h)
+        scored = (dot(q, k, 1, 1) * mask).astype(BF16)
+        d_scored = (dot(da, head(v_ref, h), 1, 1) * mask).astype(BF16)
+        dq = dot(d_scored, k, 1, 0)
         dq += rise[:, h : h + 1] * dot(da, state_ref[h].astype(BF16), 1, 1)
         dq_ref[:, here] = dq.astype(BF16)
-        dk_ref[:, here] = dot(d_scored, head(q_ref, h), 0, 0)
-        dv_ref[:, here] = dot(scored_ref[h], da, 0, 0)
+        dk_ref[:, here] = dot(d_scored, q, 0, 0)
+        dv_ref[:, here] = dot(scored, da, 0, 0)
 
 
 def final_kernel(
-    dk_local_ref, dv_local_ref, v_ref, kd_ref, ld_ref, grad_ref, dk_hbm, dv_hbm, dk_ref, dv_ref, sems
+    dk_local_ref, dv_local_ref, v_ref, kd_ref, fall_ref, grad_ref, dk_hbm, dv_hbm, dk_ref, dv_ref, sems
 ):
-    heads = ld_ref.shape[0]
-    low = triangle().astype(F32).astype(BF16)
-    cum = cum_columns(ld_ref[...], low)
-    fall = jnp.exp(cum[BLOCK - 1 : BLOCK, :] - cum)
+    heads = grad_ref.shape[0]
     copies = []
     for h in range(heads):
         here = (slice(None), slice(h * DK, (h + 1) * DK))
         grad = grad_ref[h].astype(BF16)
-        dk = head(dk_local_ref, h) + fall[:, h : h + 1] * dot(head(v_ref, h), grad, 1, 1)
+        dk = head(dk_local_ref, h) + head(fall_ref, h) * dot(head(v_ref, h), grad, 1, 1)
         dk_ref[here] = dk.astype(BF16)
         dv = head(dv_local_ref, h) + dot(head(kd_ref, h), grad, 1, 0)
         dv_ref[here] = dv.astype(BF16)
@@ -190,7 +193,7 @@
 
 
 def call(kernel, outs, flops, *args, **kinds):
-    moved = sum(a.size * a.dtype.itemsize for a in (*args, *outs))
+    moved = sum(math.prod(a.shape) * 4 for a in (*args, *outs))
     return pl.pallas_call(
         kernel,
         out_shape=outs,
@@ -217,13 +220,13 @@
     wide = heads * DK
     piece = heads * DK // ctx
     pieces = (ctx, piece, DK)
-    rows, square = (BLOCK, wide), (heads, BLOCK, BLOCK)
+    rows = (BLOCK, wide)
     unit = 2 * heads * BLOCK * DK * DK
     gain = norm_gain.reshape(1, wide)
 
-    k_decayed, packed = call(
+    packed = call(
         update_kernel,
-        (shape(rows, BF16), shape((ctx, piece + 1, 1, DK))),
+        (shape((ctx, piece + 1, 1, DK)),),
         unit,
         *(pltpu.with_memory_space_constraint(x, pltpu.HBM) for x in (key_rows, value_rows, log_decay)),
         in_specs=[IN_HBM] * 3,
@@ -231,9 +234,9 @@
             pltpu.VMEM(rows, BF16),
             pltpu.VMEM(rows, BF16),
             pltpu.VMEM(log_decay.shape, F32),
-            pltpu.SemaphoreType.DMA((2 * heads + 1,)),
+            pltpu.SemaphoreType.DMA((3,)),
         ],
-    )
+    )[0]
     packed = exchange(packed, "ctx")
     fades = packed[:, piece:, 0, :]
     before = call(
@@ -243,9 +246,9 @@
         fades,
         packed[:, :piece, 0, :],
     )[0]
-    q_decayed, scored, local, gained = call(
+    q_decayed, flipped, local, gained = call(
         local_kernel,
-        (shape(rows, BF16), shape(square, BF16), shape(rows), shape(rows)),
+        (shape(rows, BF16), shape((heads, DK, BLOCK), BF16), shape(rows), shape(rows)),
         6 * unit,
         query_rows,
         key_rows,
@@ -270,7 +273,7 @@
         (shape(rows, BF16), shape(pieces)),
         unit,
         attended,
-        q_decayed,
+        flipped,
         gained,
         sums,
     )
@@ -281,15 +284,14 @@
         fades,
         exchange(updates, "ctx"),
     )[0]
-    d_query, dk_local, dv_local = call(
+    d_query, k_decayed, fall, dk_local, dv_local = call(
         grads_kernel,
-        (shape(rows, BF16), shape(rows), shape(rows)),
-        10 * unit,
+        (shape(rows, BF16), shape(rows, BF16), shape(rows), shape(rows), shape(rows)),
+        12 * unit,
         query_rows,
         key_rows,
         value_rows,
         log_decay,
-        scored,
         states,
         d_attended,
     )
@@ -302,7 +304,7 @@
         dv_local,
         value_rows,
         k_decayed,
-        log_decay,
+        fall,
         grads,
         out_specs=(IN_HBM, IN_HBM),
         scratch_shapes=[

time: 97.5 us -> 95.6 us (0.981)
  no operation moved by 1% of the time
where the time goes in v3:
time: 95.6 us; the launch traced here: 93.9 us
  blocking collectives  58 us (61%)
  waiting for transfers between devices  17.6 us (18%)
  starting transfers between devices  9.22 us (10%)
  Pallas kernels  8.25 us (9%)
    all_to_all x3, blocking collectives, exchange(): return lax.all_to_all(array, axis, 0, 0, tiled=True)  58 us
    all_to_all x2, waiting for transfers between devices, exchange(): return lax.all_to_all(array, axis, 0, 0, tiled=True)  17.6 us
    all_to_all x2, starting transfers between devices, exchange(): return lax.all_to_all(array, axis, 0, 0, tiled=True)  9.22 us
    pallas_call x8, Pallas kernels, call(): pl.pallas_call(kernel, out_shape=outs, compiler_params=pltpu.CompilerPara...  8.25 us
  transfers between devices with their start and end apart: 2, of which 2 were waited for; matrix products, arithmetic and copies ran while one was open for 0% of the time, Pallas kernels for 3%

profile of v3, /device:TPU:1, one launch (start us, length us, event | category | flops | bytes accessed | tf_op | source)
XLA Modules:
  0.0 93.9 jit_solution(10332524814445606132)
XLA Ops:
  0.6 1.5 %shard_map.85 = f32[32,17,1,128]{3,2,1,0:T(1,128)S(1)} custom-call(bf16[256,512]{1,0:T(8,128)(2,1)} %k_ref.3, bf16[256,512]{1,0:T(8,128)(2,1)} %v_ref.5, f32[4,256]{1,0:T(4,128)} %ld_ref.3), custom_call_target="tpu_custom_call" | custom-call | flops 33554432 | bytes 1331200 | tf_op jit(solution)/shard_map/pallas_call | solution.py:197
  2.2 22.1 %all_to_all.25 = f32[32,17,1,128]{3,2,1,0:T(1,128)S(1)} all-to-all(f32[32,17,1,128]{3,2,1,0:T(1,128)S(1)} %shard_map.85), channel_id=1, replica_groups=mesh['ctx'=32,'tp'=16] {'ctx'}, dimensions={0} | all-to-all | bytes 557056 | tf_op jit(solution)/shard_map/all_to_all | solution.py:214
  24.3 0.0 copy-start.2
  24.3 0.0 copy-start.3
  24.3 0.0 copy-start.4
  24.4 0.0 copy-start.5
  24.4 0.8 shard_map.86
  25.1 0.0 copy-start
  25.1 0.0 copy-start.1
  25.1 4.6 %all-to-all-start.1 = ((f32[32,16,128]{2,1,0:T(8,128)}), f32[32,16,128]{2,1,0:T(8,128)S(1)}, u32[]{:S(2)}, u32[]{:S(2)}) async-start(f32[32,16,128]{2,1,0:T(8,128)} %shard_map.86), calls=%async_computation.1 | async-start | bytes 524288 | tf_op jit(solution)/shard_map/all_to_all | solution.py:214
  29.7 0.0 copy-done.2
  29.8 0.0 copy-done.3
  29.8 0.0 copy-done.4
  29.8 0.0 copy-done.5
  29.8 0.0 copy-done
  29.8 0.0 copy-done.1
  29.8 0.8 shard_map.87
  30.6 9.5 %all-to-all-done.1 = f32[32,16,128]{2,1,0:T(8,128)S(1)} async-done(((f32[32,16,128]{2,1,0:T(8,128)}), f32[32,16,128]{2,1,0:T(8,128)S(1)}, u32[]{:S(2)}, u32[]{:S(2)}) %all-to-all-start.1) | async-done | bytes 262176 | tf_op jit(solution)/shard_map/all_to_all | solution.py:214
  40.2 0.4 shard_map.88
  40.5 21.3 %all_to_all.26.sums_ref = f32[16,4,128]{2,1,0:T(4,128)S(1)} all-to-all(f32[16,4,128]{2,1,0:T(4,128)S(1)} %get-tuple-element.23), channel_id=1, replica_groups=mesh['ctx'=32,'tp'=16] {'tp'}, dimensions={0} | all-to-all | bytes 65536 | tf_op jit(solution)/shard_map/all_to_all | solution.py:214
  61.8 0.5 shard_map.89
  62.3 14.6 %all_to_all.27.update_ref = f32[32,16,128]{2,1,0:T(8,128)S(1)} all-to-all(f32[32,16,128]{2,1,0:T(8,128)S(1)} %get-tuple-element.30), channel_id=1, replica_groups=mesh['ctx'=32,'tp'=16] {'ctx'}, dimensions={0} | all-to-all | bytes 524288 | tf_op jit(solution)/shard_map/all_to_all | solution.py:214
  77.0 0.8 shard_map.91
  77.7 4.6 %all-to-all-start.4 = ((f32[32,16,128]{2,1,0:T(8,128)}), f32[32,16,128]{2,1,0:T(8,128)S(1)}, u32[]{:S(2)}, u32[]{:S(2)}) async-start(f32[32,16,128]{2,1,0:T(8,128)} %shard_map.91), calls=%async_computation.4 | async-start | bytes 524288 | tf_op jit(solution)/shard_map/all_to_all | solution.py:214
  82.4 2.4 %shard_map.90 = (bf16[256,512]{1,0:T(8,128)(2,1)}, bf16[256,512]{1,0:T(8,128)(2,1)S(1)}, f32[256,512]{1,0:T(8,128)S(1)}, f32[256,512]{1,0:T(8,128)S(1)}, f32[256,512]{1,0:T(8,128)S(1)}) custom-call(bf16[256,512]{1,0:T(8,128)(2,1)S(1)} %copy-done.3, bf16[256,512]{1,0:T(8,128)(2,1)S(1)} %copy-done.1, bf16[256,512]{1,0:T(8,128)(2,1)S(1)} %copy-done, ...), custom_call_target="tpu_custom_call" | custom-call | flops 402653184 | bytes 4984832 | tf_op jit(solution)/shard_map/pallas_call | solution.py:197
  84.8 8.1 %all-to-all-done.4 = f32[32,16,128]{2,1,0:T(8,128)S(1)} async-done(((f32[32,16,128]{2,1,0:T(8,128)}), f32[32,16,128]{2,1,0:T(8,128)S(1)}, u32[]{:S(2)}, u32[]{:S(2)}) %all-to-all-start.4) | async-done | bytes 262176 | tf_op jit(solution)/shard_map/all_to_all | solution.py:214
  92.9 1.0 %shard_map.92 = (bf16[256,512]{1,0:T(8,128)(2,1)}, bf16[256,512]{1,0:T(8,128)(2,1)}) custom-call(f32[256,512]{1,0:T(8,128)S(1)} %get-tuple-element.26.dk_local_ref, f32[256,512]{1,0:T(8,128)S(1)} %get-tuple-element.27.dv_local_ref, bf16[256,512]{1,0:T(8,128)(2,1)S(1)} %copy-done, bf16[256,512]{1,0:T(8,128)(2,1)S(1)} %get-tuple-element.28.kd_ref, ...), custom_call_target="tpu_custom_call" | custom-call | flops 67108864 | bytes 3932160 | tf_op jit(solution)/shard_map/pallas_call | solution.py:197
  (2 shorter events, 0.0 us)
Async XLA Ops:
  24.3 5.4 %copy-start.2 = (bf16[256,512]{1,0:T(8,128)(2,1)S(1)}, bf16[256,512]{1,0:T(8,128)(2,1)}, u32[]{:S(2)}) copy-start(bf16[256,512]{1,0:T(8,128)(2,1)} %dn_ref.1) | copy-start | bytes 786436
  24.3 5.4 %copy-start.3 = (bf16[256,512]{1,0:T(8,128)(2,1)S(1)}, bf16[256,512]{1,0:T(8,128)(2,1)}, u32[]{:S(2)}) copy-start(bf16[256,512]{1,0:T(8,128)(2,1)} %q_ref.3) | copy-start | bytes 786436
  24.3 5.4 %copy-start.4 = (f32[4,256]{1,0:T(4,128)S(1)}, f32[4,256]{1,0:T(4,128)}, u32[]{:S(2)}) copy-start(f32[4,256]{1,0:T(4,128)} %ld_ref.3) | copy-start | bytes 12292
  24.4 5.4 %copy-start.5 = (f32[512]{0:T(512)S(1)}, f32[512]{0:T(512)}, u32[]{:S(2)}) copy-start(f32[512]{0:T(512)} %param.10) | copy-start | bytes 6148
  25.1 4.6 %copy-start = (bf16[256,512]{1,0:T(8,128)(2,1)S(1)}, bf16[256,512]{1,0:T(8,128)(2,1)}, u32[]{:S(2)}) copy-start(bf16[256,512]{1,0:T(8,128)(2,1)} %v_ref.5) | copy-start | bytes 786436
  25.1 4.7 %copy-start.1 = (bf16[256,512]{1,0:T(8,128)(2,1)S(1)}, bf16[256,512]{1,0:T(8,128)(2,1)}, u32[]{:S(2)}) copy-start(bf16[256,512]{1,0:T(8,128)(2,1)} %k_ref.3) | copy-start | bytes 786436
  25.1 15.0 %all-to-all-start.1 = ((f32[32,16,128]{2,1,0:T(8,128)}), f32[32,16,128]{2,1,0:T(8,128)S(1)}, u32[]{:S(2)}, u32[]{:S(2)}) async-start(f32[32,16,128]{2,1,0:T(8,128)} %shard_map.86), calls=%async_computation.1 | async-start | bytes 524288 | tf_op jit(solution)/shard_map/all_to_all | solution.py:214
  77.7 15.1 %all-to-all-start.4 = ((f32[32,16,128]{2,1,0:T(8,128)}), f32[32,16,128]{2,1,0:T(8,128)S(1)}, u32[]{:S(2)}, u32[]{:S(2)}) async-start(f32[32,16,128]{2,1,0:T(8,128)} %shard_map.91), calls=%async_computation.4 | async-start | bytes 524288 | tf_op jit(solution)/shard_map/all_to_all | solution.py:214

commit v4 on v3

--- a/solution.py
+++ b/solution.py
@@ -100,11 +100,9 @@
         local_ref[:, here] = dot(scored.astype(BF16), head(v_ref, h), 1, 0)
 
 
-def scan_kernel(reverse, fade_ref, update_ref, before_ref):
-    size = update_ref.shape[0]
+def scan_kernel(order, fade_ref, update_ref, before_ref):
     carried = jnp.zeros(update_ref.shape[1:], F32)
-    for step in range(size):
-        at = size - 1 - step if reverse else step
+    for at in order:
         before_ref[at] = carried
         carried = carried * fade_ref[at] + update_ref[at]
 
@@ -210,8 +208,12 @@
     return jax.ShapeDtypeStruct(dims, dtype)
 
 
-def exchange(array, axis):
-    return lax.all_to_all(array, axis, 0, 0, tiled=True)
+def member_order(size, first):
+    return [(first + place) % size for place in range(size)]
+
+
+def exchange(array, axis, order):
+    return lax.all_to_all(array, axis, 0, 0, axis_index_groups=[order], tiled=True)
 
 
 def shards(query_rows, key_rows, value_rows, log_decay, norm_gain, d_normed):
@@ -223,6 +225,8 @@
     rows = (BLOCK, wide)
     unit = 2 * heads * BLOCK * DK * DK
     gain = norm_gain.reshape(1, wide)
+    order, tp_order = member_order(ctx, ctx // 2 + 2), member_order(tp, tp // 2)
+    places = [order.index(block) for block in range(ctx)]
 
     packed = call(
         update_kernel,
@@ -237,10 +241,10 @@
             pltpu.SemaphoreType.DMA((3,)),
         ],
     )[0]
-    packed = exchange(packed, "ctx")
+    packed = exchange(packed, "ctx", order)
     fades = packed[:, piece:, 0, :]
     before = call(
-        functools.partial(scan_kernel, False),
+        functools.partial(scan_kernel, places),
         (shape(pieces),),
         unit // 32,
         fades,
@@ -257,7 +261,7 @@
         gain,
         d_normed,
     )
-    states = exchange(before, "ctx").reshape(heads, DK, DK)
+    states = exchange(before, "ctx", order).reshape(heads, DK, DK)
     attended, sums = call(
         attend_kernel,
         (shape(rows, BF16), shape((tp, 4, DK))),
@@ -267,7 +271,7 @@
         states,
         gained,
     )
-    sums = exchange(sums, "tp")
+    sums = exchange(sums, "tp", tp_order)
     d_attended, updates = call(
         norm_kernel,
         (shape(rows, BF16), shape(pieces)),
@@ -278,11 +282,11 @@
         sums,
     )
     after = call(
-        functools.partial(scan_kernel, True),
+        functools.partial(scan_kernel, places[::-1]),
         (shape(pieces),),
         unit // 32,
         fades,
-        exchange(updates, "ctx"),
+        exchange(updates, "ctx", order),
     )[0]
     d_query, k_decayed, fall, dk_local, dv_local = call(
         grads_kernel,
@@ -295,7 +299,7 @@
         states,
         d_attended,
     )
-    grads = exchange(after, "ctx").reshape(heads, DK, DK)
+    grads = exchange(after, "ctx", order).reshape(heads, DK, DK)
     d_key, d_value = call(
         final_kernel,
         (shape(rows, BF16), shape(rows, BF16)),

time: 95.6 us -> 88.8 us (0.929); the launches traced: 93.9 us -> 88.3 us
  waiting for transfers between devices: 17.6 us -> 6.65 us
  starting transfers between devices: 9.22 us -> 19.6 us
  blocking collectives: 58 us -> 53 us
    all_to_all x2, waiting for transfers between devices: 17.6 us -> 6.65 us  [exchange(): lax.all_to_all(array, axis, 0, 0, axis_index_groups=[order], tiled=True)]
    all_to_all x2, starting transfers between devices: 9.22 us -> 19.6 us  [exchange(): lax.all_to_all(array, axis, 0, 0, axis_index_groups=[order], tiled=True)]
    all_to_all x3, blocking collectives: 58 us -> 53 us  [exchange(): lax.all_to_all(array, axis, 0, 0, axis_index_groups=[order], tiled=True)]
  transfers between devices with their start and end apart: 2 -> 2, of which waited for: 2 -> 2; matrix products, arithmetic and copies ran while one was open for 0% -> 0% of each run, Pallas kernels for 3% -> 4%
where the time goes in v4:
time: 88.8 us; the launch traced here: 88.3 us
  blocking collectives  53 us (60%)
  starting transfers between devices  19.6 us (22%)
  Pallas kernels  8.25 us (9%)
  waiting for transfers between devices  6.65 us (7%)
    all_to_all x3, blocking collectives, exchange(): lax.all_to_all(array, axis, 0, 0, axis_index_groups=[order], tiled=True)  53 us
    all_to_all x2, starting transfers between devices, exchange(): lax.all_to_all(array, axis, 0, 0, axis_index_groups=[order], tiled=True)  19.6 us
    pallas_call x8, Pallas kernels, call(): pl.pallas_call(kernel, out_shape=outs, compiler_params=pltpu.CompilerPara...  8.25 us
    all_to_all x2, waiting for transfers between devices, exchange(): lax.all_to_all(array, axis, 0, 0, axis_index_groups=[order], tiled=True)  6.65 us
  transfers between devices with their start and end apart: 2, of which 2 were waited for; matrix products, arithmetic and copies ran while one was open for 0% of the time, Pallas kernels for 4%

profile of v4, /device:TPU:1, one launch (start us, length us, event | category | flops | bytes accessed | tf_op | source)
XLA Modules:
  0.0 88.3 jit_solution(3636735371370949173)
XLA Ops:
  0.6 1.5 %shard_map.85 = f32[32,17,1,128]{3,2,1,0:T(1,128)S(1)} custom-call(bf16[256,512]{1,0:T(8,128)(2,1)} %k_ref.3, bf16[256,512]{1,0:T(8,128)(2,1)} %v_ref.5, f32[4,256]{1,0:T(4,128)} %ld_ref.3), custom_call_target="tpu_custom_call" | custom-call | flops 33554432 | bytes 1331200 | tf_op jit(solution)/shard_map/pallas_call | solution.py:195
  2.2 16.0 %all_to_all.25 = f32[32,17,1,128]{3,2,1,0:T(1,128)S(1)} all-to-all(f32[32,17,1,128]{3,2,1,0:T(1,128)S(1)} %shard_map.85), channel_id=1, replica_groups={{288,304,320,336,352,368,384,400,416,432,448,464,480,496,0,16,32,48,64,..., dimensions={0} | all-to-all | bytes 557056 | tf_op jit(solution)/shard_map/all_to_all | solution.py:216
  18.2 0.0 copy-start.2
  18.2 0.0 copy-start.3
  18.2 0.0 copy-start.4
  18.2 0.0 copy-start.5
  18.2 0.8 shard_map.86
  19.0 0.0 copy-start
  19.0 0.0 copy-start.1
  19.0 10.2 %all-to-all-start.1 = ((f32[32,16,128]{2,1,0:T(8,128)}), f32[32,16,128]{2,1,0:T(8,128)S(1)}, u32[]{:S(2)}, u32[]{:S(2)}) async-start(f32[32,16,128]{2,1,0:T(8,128)} %shard_map.86), calls=%async_computation.1 | async-start | bytes 524288 | tf_op jit(solution)/shard_map/all_to_all | solution.py:216
  29.2 0.0 copy-done.2
  29.2 0.0 copy-done.3
  29.3 0.0 copy-done.4
  29.3 0.0 copy-done.5
  29.3 0.0 copy-done
  29.3 0.0 copy-done.1
  29.3 0.8 shard_map.87
  30.1 3.2 %all-to-all-done.1 = f32[32,16,128]{2,1,0:T(8,128)S(1)} async-done(((f32[32,16,128]{2,1,0:T(8,128)}), f32[32,16,128]{2,1,0:T(8,128)S(1)}, u32[]{:S(2)}, u32[]{:S(2)}) %all-to-all-start.1) | async-done | bytes 262176 | tf_op jit(solution)/shard_map/all_to_all | solution.py:216
  33.3 0.4 shard_map.88
  33.7 20.8 %all_to_all.26.sums_ref = f32[16,4,128]{2,1,0:T(4,128)S(1)} all-to-all(f32[16,4,128]{2,1,0:T(4,128)S(1)} %get-tuple-element.23), channel_id=1, replica_groups={{8,9,10,11,12,13,14,15,0,1,2,3,4,5,6,7},{24,25,26,27,28,29,30,31,16,17,..., dimensions={0} | all-to-all | bytes 65536 | tf_op jit(solution)/shard_map/all_to_all | solution.py:216
  54.5 0.5 shard_map.89
  55.0 16.2 %all_to_all.27.update_ref = f32[32,16,128]{2,1,0:T(8,128)S(1)} all-to-all(f32[32,16,128]{2,1,0:T(8,128)S(1)} %get-tuple-element.30), channel_id=1, replica_groups={{288,304,320,336,352,368,384,400,416,432,448,464,480,496,0,16,32,48,64,..., dimensions={0} | all-to-all | bytes 524288 | tf_op jit(solution)/shard_map/all_to_all | solution.py:216
  71.2 0.8 shard_map.91
  72.0 9.4 %all-to-all-start.4 = ((f32[32,16,128]{2,1,0:T(8,128)}), f32[32,16,128]{2,1,0:T(8,128)S(1)}, u32[]{:S(2)}, u32[]{:S(2)}) async-start(f32[32,16,128]{2,1,0:T(8,128)} %shard_map.91), calls=%async_computation.4 | async-start | bytes 524288 | tf_op jit(solution)/shard_map/all_to_all | solution.py:216
  81.4 2.4 %shard_map.90 = (bf16[256,512]{1,0:T(8,128)(2,1)}, bf16[256,512]{1,0:T(8,128)(2,1)S(1)}, f32[256,512]{1,0:T(8,128)S(1)}, f32[256,512]{1,0:T(8,128)S(1)}, f32[256,512]{1,0:T(8,128)S(1)}) custom-call(bf16[256,512]{1,0:T(8,128)(2,1)S(1)} %copy-done.3, bf16[256,512]{1,0:T(8,128)(2,1)S(1)} %copy-done.1, bf16[256,512]{1,0:T(8,128)(2,1)S(1)} %copy-done, ...), custom_call_target="tpu_custom_call" | custom-call | flops 402653184 | bytes 4984832 | tf_op jit(solution)/shard_map/pallas_call | solution.py:195
  83.8 3.5 %all-to-all-done.4 = f32[32,16,128]{2,1,0:T(8,128)S(1)} async-done(((f32[32,16,128]{2,1,0:T(8,128)}), f32[32,16,128]{2,1,0:T(8,128)S(1)}, u32[]{:S(2)}, u32[]{:S(2)}) %all-to-all-start.4) | async-done | bytes 262176 | tf_op jit(solution)/shard_map/all_to_all | solution.py:216
  87.3 1.0 %shard_map.92 = (bf16[256,512]{1,0:T(8,128)(2,1)}, bf16[256,512]{1,0:T(8,128)(2,1)}) custom-call(f32[256,512]{1,0:T(8,128)S(1)} %get-tuple-element.26.dk_local_ref, f32[256,512]{1,0:T(8,128)S(1)} %get-tuple-element.27.dv_local_ref, bf16[256,512]{1,0:T(8,128)(2,1)S(1)} %copy-done, bf16[256,512]{1,0:T(8,128)(2,1)S(1)} %get-tuple-element.28.kd_ref, ...), custom_call_target="tpu_custom_call" | custom-call | flops 67108864 | bytes 3932160 | tf_op jit(solution)/shard_map/pallas_call | solution.py:195
  (2 shorter events, 0.0 us)
Async XLA Ops:
  18.2 11.0 %copy-start.2 = (bf16[256,512]{1,0:T(8,128)(2,1)S(1)}, bf16[256,512]{1,0:T(8,128)(2,1)}, u32[]{:S(2)}) copy-start(bf16[256,512]{1,0:T(8,128)(2,1)} %dn_ref.1) | copy-start | bytes 786436
  18.2 11.0 %copy-start.3 = (bf16[256,512]{1,0:T(8,128)(2,1)S(1)}, bf16[256,512]{1,0:T(8,128)(2,1)}, u32[]{:S(2)}) copy-start(bf16[256,512]{1,0:T(8,128)(2,1)} %q_ref.3) | copy-start | bytes 786436
  18.2 11.0 %copy-start.4 = (f32[4,256]{1,0:T(4,128)S(1)}, f32[4,256]{1,0:T(4,128)}, u32[]{:S(2)}) copy-start(f32[4,256]{1,0:T(4,128)} %ld_ref.3) | copy-start | bytes 12292
  18.2 11.0 %copy-start.5 = (f32[512]{0:T(512)S(1)}, f32[512]{0:T(512)}, u32[]{:S(2)}) copy-start(f32[512]{0:T(512)} %param.10) | copy-start | bytes 6148
  19.0 10.3 %copy-start = (bf16[256,512]{1,0:T(8,128)(2,1)S(1)}, bf16[256,512]{1,0:T(8,128)(2,1)}, u32[]{:S(2)}) copy-start(bf16[256,512]{1,0:T(8,128)(2,1)} %v_ref.5) | copy-start | bytes 786436
  19.0 10.3 %copy-start.1 = (bf16[256,512]{1,0:T(8,128)(2,1)S(1)}, bf16[256,512]{1,0:T(8,128)(2,1)}, u32[]{:S(2)}) copy-start(bf16[256,512]{1,0:T(8,128)(2,1)} %k_ref.3) | copy-start | bytes 786436
  19.0 14.3 %all-to-all-start.1 = ((f32[32,16,128]{2,1,0:T(8,128)}), f32[32,16,128]{2,1,0:T(8,128)S(1)}, u32[]{:S(2)}, u32[]{:S(2)}) async-start(f32[32,16,128]{2,1,0:T(8,128)} %shard_map.86), calls=%async_computation.1 | async-start | bytes 524288 | tf_op jit(solution)/shard_map/all_to_all | solution.py:216
  72.0 15.3 %all-to-all-start.4 = ((f32[32,16,128]{2,1,0:T(8,128)}), f32[32,16,128]{2,1,0:T(8,128)S(1)}, u32[]{:S(2)}, u32[]{:S(2)}) async-start(f32[32,16,128]{2,1,0:T(8,128)} %shard_map.91), calls=%async_computation.4 | async-start | bytes 524288 | tf_op jit(solution)/shard_map/all_to_all | solution.py:216

commit v5 on v4

--- a/solution.py
+++ b/solution.py
@@ -225,7 +225,9 @@
     rows = (BLOCK, wide)
     unit = 2 * heads * BLOCK * DK * DK
     gain = norm_gain.reshape(1, wide)
-    order, tp_order = member_order(ctx, ctx // 2 + 2), member_order(tp, tp // 2)
+    order = member_order(ctx, ctx // 2 + 2)
+    chips = member_order(tp // 2, tp // 2 - 1)
+    tp_order = [chip * 2 + core for core in (1, 0) for chip in chips]
     places = [order.index(block) for block in range(ctx)]
 
     packed = call(

time: 88.8 us -> 88.1 us (level)
  no operation moved by 1% of the time
where the time goes in v5:
time: 88.1 us; the launch traced here: 86.9 us
  blocking collectives  52.4 us (59%)
  starting transfers between devices  19.6 us (22%)
  Pallas kernels  8.25 us (9%)
  waiting for transfers between devices  5.87 us (7%)
    all_to_all x3, blocking collectives, exchange(): lax.all_to_all(array, axis, 0, 0, axis_index_groups=[order], tiled=True)  52.4 us
    all_to_all x2, starting transfers between devices, exchange(): lax.all_to_all(array, axis, 0, 0, axis_index_groups=[order], tiled=True)  19.6 us
    pallas_call x8, Pallas kernels, call(): pl.pallas_call(kernel, out_shape=outs, compiler_params=pltpu.CompilerPara...  8.25 us
    all_to_all x2, waiting for transfers between devices, exchange(): lax.all_to_all(array, axis, 0, 0, axis_index_groups=[order], tiled=True)  5.87 us
  transfers between devices with their start and end apart: 2, of which 2 were waited for; matrix products, arithmetic and copies ran while one was open for 0% of the time, Pallas kernels for 4%

profile of v5, /device:TPU:1, one launch (start us, length us, event | category | flops | bytes accessed | tf_op | source)
XLA Modules:
  0.0 86.9 jit_solution(4230488409192037041)
XLA Ops:
  0.6 1.5 %shard_map.85 = f32[32,17,1,128]{3,2,1,0:T(1,128)S(1)} custom-call(bf16[256,512]{1,0:T(8,128)(2,1)} %k_ref.3, bf16[256,512]{1,0:T(8,128)(2,1)} %v_ref.5, f32[4,256]{1,0:T(4,128)} %ld_ref.3), custom_call_target="tpu_custom_call" | custom-call | flops 33554432 | bytes 1331200 | tf_op jit(solution)/shard_map/pallas_call | solution.py:195
  2.2 16.0 %all_to_all.25 = f32[32,17,1,128]{3,2,1,0:T(1,128)S(1)} all-to-all(f32[32,17,1,128]{3,2,1,0:T(1,128)S(1)} %shard_map.85), channel_id=1, replica_groups={{288,304,320,336,352,368,384,400,416,432,448,464,480,496,0,16,32,48,64,..., dimensions={0} | all-to-all | bytes 557056 | tf_op jit(solution)/shard_map/all_to_all | solution.py:216
  18.2 0.0 copy-start.2
  18.2 0.0 copy-start.3
  18.2 0.0 copy-start.4
  18.2 0.0 copy-start.5
  18.2 0.8 shard_map.86
  19.0 0.0 copy-start
  19.0 0.0 copy-start.1
  19.0 10.2 %all-to-all-start.1 = ((f32[32,16,128]{2,1,0:T(8,128)}), f32[32,16,128]{2,1,0:T(8,128)S(1)}, u32[]{:S(2)}, u32[]{:S(2)}) async-start(f32[32,16,128]{2,1,0:T(8,128)} %shard_map.86), calls=%async_computation.1 | async-start | bytes 524288 | tf_op jit(solution)/shard_map/all_to_all | solution.py:216
  29.2 0.0 copy-done.2
  29.2 0.0 copy-done.3
  29.3 0.0 copy-done.4
  29.3 0.0 copy-done.5
  29.3 0.0 copy-done
  29.3 0.0 copy-done.1
  29.3 0.8 shard_map.87
  30.1 3.2 %all-to-all-done.1 = f32[32,16,128]{2,1,0:T(8,128)S(1)} async-done(((f32[32,16,128]{2,1,0:T(8,128)}), f32[32,16,128]{2,1,0:T(8,128)S(1)}, u32[]{:S(2)}, u32[]{:S(2)}) %all-to-all-start.1) | async-done | bytes 262176 | tf_op jit(solution)/shard_map/all_to_all | solution.py:216
  33.3 0.4 shard_map.88
  33.7 20.3 %all_to_all.26.sums_ref = f32[16,4,128]{2,1,0:T(4,128)S(1)} all-to-all(f32[16,4,128]{2,1,0:T(4,128)S(1)} %get-tuple-element.23), channel_id=1, replica_groups={{15,1,3,5,7,9,11,13,14,0,2,4,6,8,10,12},{31,17,19,21,23,25,27,29,30,16,..., dimensions={0} | all-to-all | bytes 65536 | tf_op jit(solution)/shard_map/all_to_all | solution.py:216
  54.0 0.5 shard_map.89
  54.5 16.0 %all_to_all.27.update_ref = f32[32,16,128]{2,1,0:T(8,128)S(1)} all-to-all(f32[32,16,128]{2,1,0:T(8,128)S(1)} %get-tuple-element.30), channel_id=1, replica_groups={{288,304,320,336,352,368,384,400,416,432,448,464,480,496,0,16,32,48,64,..., dimensions={0} | all-to-all | bytes 524288 | tf_op jit(solution)/shard_map/all_to_all | solution.py:216
  70.6 0.8 shard_map.91
  71.3 9.4 %all-to-all-start.4 = ((f32[32,16,128]{2,1,0:T(8,128)}), f32[32,16,128]{2,1,0:T(8,128)S(1)}, u32[]{:S(2)}, u32[]{:S(2)}) async-start(f32[32,16,128]{2,1,0:T(8,128)} %shard_map.91), calls=%async_computation.4 | async-start | bytes 524288 | tf_op jit(solution)/shard_map/all_to_all | solution.py:216
  80.7 2.4 %shard_map.90 = (bf16[256,512]{1,0:T(8,128)(2,1)}, bf16[256,512]{1,0:T(8,128)(2,1)S(1)}, f32[256,512]{1,0:T(8,128)S(1)}, f32[256,512]{1,0:T(8,128)S(1)}, f32[256,512]{1,0:T(8,128)S(1)}) custom-call(bf16[256,512]{1,0:T(8,128)(2,1)S(1)} %copy-done.3, bf16[256,512]{1,0:T(8,128)(2,1)S(1)} %copy-done.1, bf16[256,512]{1,0:T(8,128)(2,1)S(1)} %copy-done, ...), custom_call_target="tpu_custom_call" | custom-call | flops 402653184 | bytes 4984832 | tf_op jit(solution)/shard_map/pallas_call | solution.py:195
  83.1 2.7 %all-to-all-done.4 = f32[32,16,128]{2,1,0:T(8,128)S(1)} async-done(((f32[32,16,128]{2,1,0:T(8,128)}), f32[32,16,128]{2,1,0:T(8,128)S(1)}, u32[]{:S(2)}, u32[]{:S(2)}) %all-to-all-start.4) | async-done | bytes 262176 | tf_op jit(solution)/shard_map/all_to_all | solution.py:216
  85.9 1.0 %shard_map.92 = (bf16[256,512]{1,0:T(8,128)(2,1)}, bf16[256,512]{1,0:T(8,128)(2,1)}) custom-call(f32[256,512]{1,0:T(8,128)S(1)} %get-tuple-element.26.dk_local_ref, f32[256,512]{1,0:T(8,128)S(1)} %get-tuple-element.27.dv_local_ref, bf16[256,512]{1,0:T(8,128)(2,1)S(1)} %copy-done, bf16[256,512]{1,0:T(8,128)(2,1)S(1)} %get-tuple-element.28.kd_ref, ...), custom_call_target="tpu_custom_call" | custom-call | flops 67108864 | bytes 3932160 | tf_op jit(solution)/shard_map/pallas_call | solution.py:195
  (2 shorter events, 0.0 us)
Async XLA Ops:
  18.2 11.0 %copy-start.2 = (bf16[256,512]{1,0:T(8,128)(2,1)S(1)}, bf16[256,512]{1,0:T(8,128)(2,1)}, u32[]{:S(2)}) copy-start(bf16[256,512]{1,0:T(8,128)(2,1)} %dn_ref.1) | copy-start | bytes 786436
  18.2 11.0 %copy-start.3 = (bf16[256,512]{1,0:T(8,128)(2,1)S(1)}, bf16[256,512]{1,0:T(8,128)(2,1)}, u32[]{:S(2)}) copy-start(bf16[256,512]{1,0:T(8,128)(2,1)} %q_ref.3) | copy-start | bytes 786436
  18.2 11.0 %copy-start.4 = (f32[4,256]{1,0:T(4,128)S(1)}, f32[4,256]{1,0:T(4,128)}, u32[]{:S(2)}) copy-start(f32[4,256]{1,0:T(4,128)} %ld_ref.3) | copy-start | bytes 12292
  18.2 11.0 %copy-start.5 = (f32[512]{0:T(512)S(1)}, f32[512]{0:T(512)}, u32[]{:S(2)}) copy-start(f32[512]{0:T(512)} %param.10) | copy-start | bytes 6148
  19.0 10.3 %copy-start = (bf16[256,512]{1,0:T(8,128)(2,1)S(1)}, bf16[256,512]{1,0:T(8,128)(2,1)}, u32[]{:S(2)}) copy-start(bf16[256,512]{1,0:T(8,128)(2,1)} %v_ref.5) | copy-start | bytes 786436
  19.0 10.3 %copy-start.1 = (bf16[256,512]{1,0:T(8,128)(2,1)S(1)}, bf16[256,512]{1,0:T(8,128)(2,1)}, u32[]{:S(2)}) copy-start(bf16[256,512]{1,0:T(8,128)(2,1)} %k_ref.3) | copy-start | bytes 786436
  19.0 14.3 %all-to-all-start.1 = ((f32[32,16,128]{2,1,0:T(8,128)}), f32[32,16,128]{2,1,0:T(8,128)S(1)}, u32[]{:S(2)}, u32[]{:S(2)}) async-start(f32[32,16,128]{2,1,0:T(8,128)} %shard_map.86), calls=%async_computation.1 | async-start | bytes 524288 | tf_op jit(solution)/shard_map/all_to_all | solution.py:216
  71.3 14.5 %all-to-all-start.4 = ((f32[32,16,128]{2,1,0:T(8,128)}), f32[32,16,128]{2,1,0:T(8,128)S(1)}, u32[]{:S(2)}, u32[]{:S(2)}) async-start(f32[32,16,128]{2,1,0:T(8,128)} %shard_map.91), calls=%async_computation.4 | async-start | bytes 524288 | tf_op jit(solution)/shard_map/all_to_all | solution.py:216

commit v6 on v5

--- a/solution.py
+++ b/solution.py
@@ -225,8 +225,8 @@
     rows = (BLOCK, wide)
     unit = 2 * heads * BLOCK * DK * DK
     gain = norm_gain.reshape(1, wide)
-    order = member_order(ctx, ctx // 2 + 2)
-    chips = member_order(tp // 2, tp // 2 - 1)
+    order = member_order(ctx, ctx // 2 + 6)
+    chips = member_order(tp // 2, tp // 2 - 2)
     tp_order = [chip * 2 + core for core in (1, 0) for chip in chips]
     places = [order.index(block) for block in range(ctx)]
 

time: 88.1 us -> 88.2 us (level)
  the two profiles are of different devices: /device:TPU:1 before, /device:TPU:2 now
where the time goes in v6:
time: 88.2 us; the launch traced here: 87.8 us
  blocking collectives  50.6 us (57%)
  starting transfers between devices  16.7 us (19%)
  waiting for transfers between devices  11.4 us (13%)
  Pallas kernels  8.25 us (9%)
    all_to_all x3, blocking collectives, exchange(): lax.all_to_all(array, axis, 0, 0, axis_index_groups=[order], tiled=True)  50.6 us
    all_to_all x2, starting transfers between devices, exchange(): lax.all_to_all(array, axis, 0, 0, axis_index_groups=[order], tiled=True)  16.7 us
    all_to_all x2, waiting for transfers between devices, exchange(): lax.all_to_all(array, axis, 0, 0, axis_index_groups=[order], tiled=True)  11.4 us
    pallas_call x8, Pallas kernels, call(): pl.pallas_call(kernel, out_shape=outs, compiler_params=pltpu.CompilerPara...  8.25 us
  transfers between devices with their start and end apart: 2, of which 2 were waited for; matrix products, arithmetic and copies ran while one was open for 0% of the time, Pallas kernels for 4%

profile of v6, /device:TPU:2, one launch (start us, length us, event | category | flops | bytes accessed | tf_op | source)
XLA Modules:
  0.0 87.8 jit_solution(5005256493414552316)
XLA Ops:
  0.6 1.5 %shard_map.85 = f32[32,17,1,128]{3,2,1,0:T(1,128)S(1)} custom-call(bf16[256,512]{1,0:T(8,128)(2,1)} %k_ref.3, bf16[256,512]{1,0:T(8,128)(2,1)} %v_ref.5, f32[4,256]{1,0:T(4,128)} %ld_ref.3), custom_call_target="tpu_custom_call" | custom-call | flops 33554432 | bytes 1331200 | tf_op jit(solution)/shard_map/pallas_call | solution.py:195
  2.2 20.0 %all_to_all.25 = f32[32,17,1,128]{3,2,1,0:T(1,128)S(1)} all-to-all(f32[32,17,1,128]{3,2,1,0:T(1,128)S(1)} %shard_map.85), channel_id=1, replica_groups={{352,368,384,400,416,432,448,464,480,496,0,16,32,48,64,80,96,112,128,14..., dimensions={0} | all-to-all | bytes 557056 | tf_op jit(solution)/shard_map/all_to_all | solution.py:216
  22.2 0.0 copy-start.2
  22.2 0.0 copy-start.3
  22.3 0.0 copy-start.4
  22.3 0.0 copy-start.5
  22.3 0.8 shard_map.86
  23.1 0.0 copy-start
  23.1 0.0 copy-start.1
  23.1 8.3 %all-to-all-start.1 = ((f32[32,16,128]{2,1,0:T(8,128)}), f32[32,16,128]{2,1,0:T(8,128)S(1)}, u32[]{:S(2)}, u32[]{:S(2)}) async-start(f32[32,16,128]{2,1,0:T(8,128)} %shard_map.86), calls=%async_computation.1 | async-start | bytes 524288 | tf_op jit(solution)/shard_map/all_to_all | solution.py:216
  31.3 0.0 copy-done.2
  31.3 0.0 copy-done.3
  31.3 0.0 copy-done.4
  31.4 0.0 copy-done.5
  31.4 0.0 copy-done
  31.4 0.0 copy-done.1
  31.4 0.8 shard_map.87
  32.2 6.5 %all-to-all-done.1 = f32[32,16,128]{2,1,0:T(8,128)S(1)} async-done(((f32[32,16,128]{2,1,0:T(8,128)}), f32[32,16,128]{2,1,0:T(8,128)S(1)}, u32[]{:S(2)}, u32[]{:S(2)}) %all-to-all-start.1) | async-done | bytes 262176 | tf_op jit(solution)/shard_map/all_to_all | solution.py:216
  38.7 0.4 shard_map.88
  39.1 14.1 %all_to_all.26.sums_ref = f32[16,4,128]{2,1,0:T(4,128)S(1)} all-to-all(f32[16,4,128]{2,1,0:T(4,128)S(1)} %get-tuple-element.23), channel_id=1, replica_groups={{13,15,1,3,5,7,9,11,12,14,0,2,4,6,8,10},{29,31,17,19,21,23,25,27,28,30,..., dimensions={0} | all-to-all | bytes 65536 | tf_op jit(solution)/shard_map/all_to_all | solution.py:216
  53.2 0.5 shard_map.89
  53.8 16.4 %all_to_all.27.update_ref = f32[32,16,128]{2,1,0:T(8,128)S(1)} all-to-all(f32[32,16,128]{2,1,0:T(8,128)S(1)} %get-tuple-element.30), channel_id=1, replica_groups={{352,368,384,400,416,432,448,464,480,496,0,16,32,48,64,80,96,112,128,14..., dimensions={0} | all-to-all | bytes 524288 | tf_op jit(solution)/shard_map/all_to_all | solution.py:216
  70.2 0.8 shard_map.91
  70.9 8.5 %all-to-all-start.4 = ((f32[32,16,128]{2,1,0:T(8,128)}), f32[32,16,128]{2,1,0:T(8,128)S(1)}, u32[]{:S(2)}, u32[]{:S(2)}) async-start(f32[32,16,128]{2,1,0:T(8,128)} %shard_map.91), calls=%async_computation.4 | async-start | bytes 524288 | tf_op jit(solution)/shard_map/all_to_all | solution.py:216
  79.4 2.4 %shard_map.90 = (bf16[256,512]{1,0:T(8,128)(2,1)}, bf16[256,512]{1,0:T(8,128)(2,1)S(1)}, f32[256,512]{1,0:T(8,128)S(1)}, f32[256,512]{1,0:T(8,128)S(1)}, f32[256,512]{1,0:T(8,128)S(1)}) custom-call(bf16[256,512]{1,0:T(8,128)(2,1)S(1)} %copy-done.3, bf16[256,512]{1,0:T(8,128)(2,1)S(1)} %copy-done.1, bf16[256,512]{1,0:T(8,128)(2,1)S(1)} %copy-done, ...), custom_call_target="tpu_custom_call" | custom-call | flops 402653184 | bytes 4984832 | tf_op jit(solution)/shard_map/pallas_call | solution.py:195
  81.8 4.9 %all-to-all-done.4 = f32[32,16,128]{2,1,0:T(8,128)S(1)} async-done(((f32[32,16,128]{2,1,0:T(8,128)}), f32[32,16,128]{2,1,0:T(8,128)S(1)}, u32[]{:S(2)}, u32[]{:S(2)}) %all-to-all-start.4) | async-done | bytes 262176 | tf_op jit(solution)/shard_map/all_to_all | solution.py:216
  86.8 1.0 %shard_map.92 = (bf16[256,512]{1,0:T(8,128)(2,1)}, bf16[256,512]{1,0:T(8,128)(2,1)}) custom-call(f32[256,512]{1,0:T(8,128)S(1)} %get-tuple-element.26.dk_local_ref, f32[256,512]{1,0:T(8,128)S(1)} %get-tuple-element.27.dv_local_ref, bf16[256,512]{1,0:T(8,128)(2,1)S(1)} %copy-done, bf16[256,512]{1,0:T(8,128)(2,1)S(1)} %get-tuple-element.28.kd_ref, ...), custom_call_target="tpu_custom_call" | custom-call | flops 67108864 | bytes 3932160 | tf_op jit(solution)/shard_map/pallas_call | solution.py:195
  (2 shorter events, 0.0 us)
Async XLA Ops:
  22.2 9.1 %copy-start.2 = (bf16[256,512]{1,0:T(8,128)(2,1)S(1)}, bf16[256,512]{1,0:T(8,128)(2,1)}, u32[]{:S(2)}) copy-start(bf16[256,512]{1,0:T(8,128)(2,1)} %dn_ref.1) | copy-start | bytes 786436
  22.2 9.1 %copy-start.3 = (bf16[256,512]{1,0:T(8,128)(2,1)S(1)}, bf16[256,512]{1,0:T(8,128)(2,1)}, u32[]{:S(2)}) copy-start(bf16[256,512]{1,0:T(8,128)(2,1)} %q_ref.3) | copy-start | bytes 786436
  22.3 9.1 %copy-start.4 = (f32[4,256]{1,0:T(4,128)S(1)}, f32[4,256]{1,0:T(4,128)}, u32[]{:S(2)}) copy-start(f32[4,256]{1,0:T(4,128)} %ld_ref.3) | copy-start | bytes 12292
  22.3 9.1 %copy-start.5 = (f32[512]{0:T(512)S(1)}, f32[512]{0:T(512)}, u32[]{:S(2)}) copy-start(f32[512]{0:T(512)} %param.10) | copy-start | bytes 6148
  23.1 8.3 %copy-start = (bf16[256,512]{1,0:T(8,128)(2,1)S(1)}, bf16[256,512]{1,0:T(8,128)(2,1)}, u32[]{:S(2)}) copy-start(bf16[256,512]{1,0:T(8,128)(2,1)} %v_ref.5) | copy-start | bytes 786436
  23.1 8.3 %copy-start.1 = (bf16[256,512]{1,0:T(8,128)(2,1)S(1)}, bf16[256,512]{1,0:T(8,128)(2,1)}, u32[]{:S(2)}) copy-start(bf16[256,512]{1,0:T(8,128)(2,1)} %k_ref.3) | copy-start | bytes 786436
  23.1 15.7 %all-to-all-start.1 = ((f32[32,16,128]{2,1,0:T(8,128)}), f32[32,16,128]{2,1,0:T(8,128)S(1)}, u32[]{:S(2)}, u32[]{:S(2)}) async-start(f32[32,16,128]{2,1,0:T(8,128)} %shard_map.86), calls=%async_computation.1 | async-start | bytes 524288 | tf_op jit(solution)/shard_map/all_to_all | solution.py:216
  70.9 15.8 %all-to-all-start.4 = ((f32[32,16,128]{2,1,0:T(8,128)}), f32[32,16,128]{2,1,0:T(8,128)S(1)}, u32[]{:S(2)}, u32[]{:S(2)}) async-start(f32[32,16,128]{2,1,0:T(8,128)} %shard_map.91), calls=%async_computation.4 | async-start | bytes 524288 | tf_op jit(solution)/shard_map/all_to_all | solution.py:216
